TPU v7x, 32 devices: a whole 2x2x4 slice. The times are simulated.
32 devices in a mesh: ctx: 8 (over z, x), head: 4 (over y, core).
Axes of the slice: x: 2, y: 2, z: 4, core: 2. Of those that a mesh axis runs over, the one named last changes fastest.
Arguments:
- feat_in: bfloat16 [2048, 8192], P('ctx', 'head'), may hold values from -6 to 6
- gate_in: bfloat16 [2048, 8192], P('ctx', 'head'), may hold values from -6 to 6
- state_proj: bfloat16 [2048, 256], P('ctx'), may hold values from -1.5 to 1.5
- step_raw: float32 [64, 2048], P('head', 'ctx'), may hold values from -6 to 6
- doc_offset: int32 [2048], P('ctx'), may hold values from 0 to 511, as said below
- feat_taps: float32 [4, 8192], P(None, 'head'), may hold values from -3 to 3
- feat_bias: float32 [8192], P('head'), may hold values from -1.5 to 1.5
- proj_taps: float32 [4, 256], replicated, may hold values from -3 to 3
- proj_bias: float32 [256], replicated, may hold values from -0.6 to 0.6
- step_bias: float32 [64], P('head'), may hold values from -4 to -1
- decay_log: float32 [64], P('head'), may hold values from -13 to -0.7
- skip_gain: float32 [64], P('head'), may hold values from 0.5 to 1.5
- norm_gain: float32 [8192], P('head'), may hold values from 0.1 to 1.9
Outputs:
- mixer_out: bfloat16 [2048, 8192], P('ctx', 'head')
Inputs may be any that keep to these rules, and one draw needn't show every extreme that they name: `doc_offset`: the position of each token within its document: 0 at a document's first token, rising by one per token inside it. A document holds at most 512 tokens, and every document but the window's last holds more than 64.
All inputs are finite; a program needn't handle non-finite values.
Results may differ from a plain program's by a relative error of at most 0.006.
Values may be sent and summed in bfloat16 or wider, within the bound.
A program may use at most 64 MiB of HBM per device.

v0:
```python
import functools

import jax
import jax.numpy as jnp
from jax import lax
from jax.experimental import pallas as pl
from jax.experimental.pallas import tpu as pltpu
from jax.sharding import PartitionSpec as P


def passed_along(block, axis, distance):
    devices = range(lax.axis_size(axis))
    route = [(i - distance, i) for i in devices if i - distance in devices]
    return lax.ppermute(block, axis, route)


def causal_taps(values, rim_rows, kernel_taps, kernel_bias, offsets):
    row_count = values.shape[0]
    tap_count = kernel_taps.shape[0]
    joined = jnp.concatenate([rim_rows, values], axis=0).astype(jnp.float32)
    summed = jnp.broadcast_to(kernel_bias[None, :], values.shape)
    for tap_index in range(tap_count):
        tap_lag = tap_count - 1 - tap_index
        window_rows = lax.slice_in_dim(joined, tap_index, tap_index + row_count, axis=0)
        summed = summed + jnp.where(
            (offsets >= tap_lag)[:, None], kernel_taps[tap_index][None, :] * window_rows, 0.0
        )
    return jax.nn.silu(summed).astype(jnp.bfloat16)


def combine_states(earlier_part, later_part):
    return (
        earlier_part[0] * later_part[0],
        later_part[0][:, None, None] * earlier_part[1] + later_part[1],
    )


def body(
    feat_in,
    gate_in,
    state_proj,
    step_raw,
    doc_offset,
    feat_taps,
    feat_bias,
    proj_taps,
    proj_bias,
    step_bias,
    decay_log,
    skip_gain,
    norm_gain,
):
    head_count = step_raw.shape[0]
    row_count = feat_in.shape[0]
    head_dim = feat_in.shape[1] // head_count
    state_size = state_proj.shape[1] // 2
    tap_count = feat_taps.shape[0]
    rim_feat, rim_proj = passed_along(
        (feat_in[row_count - tap_count + 1 :], state_proj[row_count - tap_count + 1 :]), "ctx", 1
    )
    conv_feat = causal_taps(feat_in, rim_feat, feat_taps, feat_bias, doc_offset)
    conv_proj = causal_taps(state_proj, rim_proj, proj_taps, proj_bias, doc_offset)
    step_all = jax.nn.softplus(step_raw + step_bias[:, None])
    rate_all = step_all * (-jnp.exp(decay_log))[:, None]
    block_rows = min(512, row_count)
    position = jnp.arange(block_rows, dtype=jnp.int32)
    causal = position[None, :] <= position[:, None]
    final_row = block_rows - 1
    element_decay = jnp.ones((head_count,), jnp.float32)
    element_state = jnp.zeros((head_count, head_dim, state_size), jnp.float32)
    block_index = 0
    start = block_index * block_rows
    feat_block = conv_feat.reshape(block_rows, head_count, head_dim)
    in_block = conv_proj[start : start + block_rows, :state_size]
    out_block = conv_proj[start : start + block_rows, state_size:]
    cumulative = jnp.cumsum(rate_all, axis=1)
    same_doc = causal & (doc_offset[:, None] >= position[:, None] - position[None, :])
    scores = jnp.dot(out_block, in_block.T, preferred_element_type=jnp.float32)
    exponent_gap = jnp.where(
        same_doc[None], cumulative[:, :, None] - cumulative[:, None, :], -jnp.inf
    )
    weights = (scores[None] * jnp.exp(exponent_gap) * step_all[:, None, :]).astype(jnp.bfloat16)
    inner_out = jnp.einsum("hts,shp->thp", weights, feat_block, preferred_element_type=jnp.float32)
    reaches = doc_offset >= position + 1
    tail_mask = doc_offset[final_row] >= final_row - position
    tail_coef = jnp.where(
        tail_mask[None, :],
        jnp.exp(cumulative[:, final_row : final_row + 1] - cumulative) * step_all,
        0.0,
    )
    scaled = (in_block.astype(jnp.float32)[None] * tail_coef[:, :, None]).astype(jnp.bfloat16)
    contrib = jnp.einsum("shp,hsn->hpn", feat_block, scaled, preferred_element_type=jnp.float32)
    keep_factor = jnp.where(reaches[final_row], jnp.exp(cumulative[:, final_row]), 0.0)
    saved_blocks = [(feat_block, out_block, cumulative, reaches, inner_out, contrib, keep_factor)]
    element_state = keep_factor[:, None, None] * element_state + contrib
    element_decay = element_decay * keep_factor
    longest_doc = row_count * lax.axis_size("ctx") // 4
    span_back = (longest_doc + row_count - 2) // row_count
    distances = [1]
    window_size = 1
    while window_size < span_back:
        distances.append(window_size)
        window_size = window_size * 2
    current = (element_decay, element_state)
    for turn_index, distance in enumerate(distances):
        moved = passed_along((current[0], current[1]), "ctx", distance)
        if turn_index == 0:
            current = moved
        else:
            current = combine_states(moved, current)
    start_state = current[1]
    pieces_out = []
    for block_index, saved in enumerate(saved_blocks):
        feat_block, out_block, cumulative, reaches, inner_out, contrib, keep_factor = saved
        lift_factor = jnp.where(reaches[None, :], jnp.exp(cumulative), 0.0)
        from_state = (
            jnp.einsum(
                "tn,hpn->thp",
                out_block.astype(jnp.float32),
                start_state,
                precision=lax.Precision.HIGHEST,
            )
            * lift_factor.T[:, :, None]
        )
        pieces_out.append(
            inner_out + from_state + skip_gain[None, :, None] * feat_block.astype(jnp.float32)
        )
    mixed = pieces_out[0].reshape(row_count, head_count * head_dim)
    gated = mixed * jax.nn.silu(gate_in.astype(jnp.float32))
    squares = jnp.sum(gated * gated, axis=1)
    total_squares = lax.psum(squares, "head")
    scale = lax.rsqrt(total_squares / (head_count * head_dim * lax.axis_size("head")) + 1e-05)
    return (gated * scale[:, None] * norm_gain[None, :]).astype(jnp.bfloat16)


PAIR = 2
LAG = 2
EARLY = 8
GATED = jnp.bfloat16

LOG2E = 1.4426950408889634
F32 = jnp.float32
BF16 = jnp.bfloat16
EXACT = lax.Precision.HIGHEST


def to_column(row, size):
    rows = lax.broadcasted_iota(jnp.int32, (size, size), 0)
    cols = lax.broadcasted_iota(jnp.int32, (size, size), 1)
    return jnp.sum(jnp.where(rows == cols, row, 0.0), axis=1, keepdims=True)


def tap_sum(window_of, taps, bias, offsets, tap_count):
    summed = bias
    for tap_index in range(tap_count):
        tap_lag = tap_count - 1 - tap_index
        term = taps[tap_index : tap_index + 1, :] * window_of(tap_lag)
        if tap_lag:
            term = jnp.where(offsets >= float(tap_lag), term, 0.0)
        summed = summed + term
    return summed * (1.0 / (1.0 + jnp.exp(-summed)))


def mixer_kernel(
    ctx_size, head_size, pair,
    feat_hbm, gate_hbm, proj_hbm, step_ref, offset_ref, offset_smem, taps_ref, bias_ref,
    ptaps_ref, pbias_ref, sbias_ref, dlog_ref, skip_smem,
    gated_hbm, scale_ref,
    feat, gate, proj, xs, xp, rim, prim, conv, in_t, bc, out_b, masked, cb, a_rows, coef,
    offs, own, send, arecv, srecv, sout, lsend, lrecv, kown, kin, yv, g2, gated, part, sq, sqr,
    feat_sems, gate_sems, out_sems, proj_sem, halo_send, halo_recv, keep_sems,
    asend, arecv_sem, ssend, srecv_sem, fsend, lrecv_sem, sqsend, sqrecv,
):
    d = lax.axis_index("ctx")
    hd = lax.axis_index("head")
    rows, cols = feat.shape
    heads = step_ref.shape[0]
    hdim = cols // heads
    state = in_t.shape[0]
    taps_n = taps_ref.shape[0]
    width = pair * hdim
    chunks = heads // pair
    half = rows // 2
    odd = d % 2 == 1
    even = d % 2 == 0
    parity = d % 2
    mate = d + 1 - 2 * parity
    part_chunks = heads // pair // 2
    mine = parity * part_chunks
    theirs = part_chunks - mine
    sends_early = even | (d + 1 < ctx_size)
    gets_early = odd | (d + 2 < ctx_size)
    sends_late = even | (d >= 2)
    gets_late = odd | (d >= 2)

    def chunk_cols(c):
        return pl.ds(pl.multiple_of(c * width, width), width)

    def feat_copy(c):
        return pltpu.make_async_copy(feat_hbm.at[:, chunk_cols(c)], feat.at[:, chunk_cols(c)], feat_sems.at[c])

    def gate_copy(c):
        return pltpu.make_async_copy(gate_hbm.at[:, chunk_cols(c)], gate.at[:, chunk_cols(c)], gate_sems.at[c])

    def out_copy(c):
        return pltpu.make_async_copy(gated.at[:, chunk_cols(c)], gated_hbm.at[:, chunk_cols(c)], out_sems.at[c])

    def remote(src, dst, ssem, rsem, where):
        return pltpu.make_async_remote_copy(
            src_ref=src, dst_ref=dst, send_sem=ssem, recv_sem=rsem,
            device_id=where, device_id_type=pl.DeviceIdType.MESH,
        )

    barrier = pltpu.get_barrier_semaphore()
    for shift in (-2, -1, 1, 2):
        @pl.when((d + shift >= 0) & (d + shift < ctx_size))
        def _():
            pl.semaphore_signal(barrier, inc=1, device_id=(d + shift, hd), device_id_type=pl.DeviceIdType.MESH)
    for k in range(1, head_size):
        pl.semaphore_signal(
            barrier, inc=1, device_id=(d, lax.rem(hd + k, head_size)), device_id_type=pl.DeviceIdType.MESH
        )

    proj_copy = pltpu.make_async_copy(proj_hbm, proj, proj_sem)
    proj_copy.start()
    for c in range(chunks):
        feat_copy(c).start()
    for c in range(chunks):
        gate_copy(c).start()

    off_col = to_column(offset_ref[...].astype(F32), rows)
    offs[...] = jnp.broadcast_to(off_col, offs.shape)
    step = jax.nn.softplus(step_ref[...] + to_column(sbias_ref[...], heads))
    rate = step * (-jnp.exp(to_column(dlog_ref[...], heads)) * LOG2E)
    near = jnp.minimum(d, 2) + jnp.minimum(ctx_size - 1 - d, 2) + head_size - 1
    pl.semaphore_wait(barrier, near)
    halo_f = remote(feat_hbm.at[pl.ds(rows - 8, 8), :], rim, halo_send.at[0], halo_recv.at[0], (d + 1, hd))
    halo_p = remote(proj_hbm.at[pl.ds(rows - 8, 8), :], prim, halo_send.at[1], halo_recv.at[1], (d + 1, hd))

    @pl.when(d + 1 < ctx_size)
    def _():
        halo_p.start()
        halo_f.start()

    @pl.when(d == 0)
    def _():
        rim[...] = jnp.zeros_like(rim)
        prim[...] = jnp.zeros_like(prim)

    @pl.when(d < 2)
    def _():
        srecv[...] = jnp.zeros_like(srecv)

    @pl.when(d == 0)
    def _():
        lrecv[...] = jnp.zeros_like(lrecv)

    upper = (
        lax.broadcasted_iota(jnp.int32, (rows, rows), 0) <= lax.broadcasted_iota(jnp.int32, (rows, rows), 1)
    ).astype(F32)
    cum = jnp.dot(rate, upper, precision=EXACT, preferred_element_type=F32)
    shifted = cum - jnp.log(step) * LOG2E
    a_rows[...] = shifted
    last = offset_smem[rows - 1]
    place = lax.broadcasted_iota(jnp.int32, (heads, rows), 1)
    coef[...] = jnp.where(last >= rows - 1 - place, jnp.exp2(cum[:, rows - 1 : rows] - shifted), 0.0)
    keep = jnp.where(last >= rows, jnp.exp2(cum[:, rows - 1 : rows]), 0.0)
    cum_t = cum.T
    for h in range(heads):
        cb[h] = jnp.broadcast_to(cum_t[:, h : h + 1], (rows, hdim))
        kown[:, h * hdim : (h + 1) * hdim] = jnp.broadcast_to(keep[h : h + 1, :], (1, hdim))

    keep_msg = remote(kown, kin, keep_sems.at[0], keep_sems.at[1], (mate, hd))
    keep_msg.start()

    def conv_main(c):
        feat_copy(c).wait()
        sl = chunk_cols(c)
        xs[8:, sl] = feat[:, sl].astype(F32)
        conv[16:, sl] = tap_sum(
            lambda lag: xs[24 - lag : 8 + rows - lag, sl], taps_ref[:, sl], bias_ref[:, sl], offs[16:, :1], taps_n
        ).astype(BF16)

    def conv_top(c):
        sl = chunk_cols(c)
        xs[:8, sl] = rim[:, sl].astype(F32)
        conv[:16, sl] = tap_sum(
            lambda lag: xs[8 - lag : 24 - lag, sl], taps_ref[:, sl], bias_ref[:, sl], offs[:16, :1], taps_n
        ).astype(BF16)

    def ordered(i):
        return lax.rem(mine + i, chunks)

    def early_body(c, _):
        conv_main(ordered(c))
        return 0

    proj_copy.wait()
    xp[8:, :] = proj[...].astype(F32)
    cp = tap_sum(
        lambda lag: xp[24 - lag : 8 + rows - lag, :], ptaps_ref[...], pbias_ref[...], offs[16:, :1], taps_n
    ).astype(BF16)
    bc[16:, :] = cp
    lax.fori_loop(0, min(EARLY // pair, chunks), early_body, 0)

    @pl.when(d > 0)
    def _():
        halo_p.wait_recv()
        halo_f.wait_recv()

    xp[:8, :] = prim[...].astype(F32)
    bc[:16, :] = tap_sum(
        lambda lag: xp[8 - lag : 24 - lag, :], ptaps_ref[...], pbias_ref[...], offs[:16, :1], taps_n
    ).astype(BF16)
    in_b = bc[:, :state]
    in_t[...] = in_b.astype(F32).T
    out_b[...] = bc[:, state:]

    def contrib(c):
        conv_top(c)
        for k in range(pair):
            h = c * pair + k
            scaled = (in_t[...] * coef[pl.ds(h, 1), :]).astype(BF16)
            fcols = pl.ds(pl.multiple_of(h * hdim, hdim), hdim)
            got = jnp.dot(scaled, conv[:, fcols], preferred_element_type=F32)
            own[c, :, k * hdim : (k + 1) * hdim] = got
            send[c, :, k * hdim : (k + 1) * hdim] = got.astype(BF16)

        @pl.when(sends_early & (c >= mine) & (c < mine + part_chunks))
        def _():
            a_copy(c - mine).start()

    def contrib_body(i, _):
        contrib(ordered(i))
        return 0

    def late_body(i, _):
        conv_main(ordered(i))
        contrib(ordered(i))
        return 0

    def a_copy(r):
        return remote(send.at[mine + r], arecv.at[r], asend.at[r], arecv_sem.at[r], (mate, hd))

    def s_copy(r):
        return remote(sout.at[r], srecv.at[r], ssend.at[r], srecv_sem.at[r], (d + 2, hd))

    def f_copy(r):
        return remote(lsend.at[r], lrecv.at[r], fsend.at[r], lrecv_sem.at[r], (mate, hd))

    def g_copy(r):
        return remote(srecv.at[r], lrecv.at[r], fsend.at[r], lrecv_sem.at[r], (mate, hd))

    lax.fori_loop(0, min(EARLY // pair, chunks), contrib_body, 0)
    lax.fori_loop(min(EARLY // pair, chunks), chunks, late_body, 0)
    scores = lax.dot_general(out_b[...], in_b, (((1,), (1,)), ((), ())), preferred_element_type=F32)
    ti = lax.broadcasted_iota(jnp.int32, (rows, rows), 0)
    si = lax.broadcasted_iota(jnp.int32, (rows, rows), 1)
    gap = ti - si
    masked[...] = jnp.where((gap >= 0) & (offs[:, :1] >= gap.astype(F32)), scores, 0.0)
    part[...] = jnp.zeros_like(part)

    def local_part(c):
        gate_copy(c).wait()
        for k in range(pair):
            h = c * pair + k
            fcols = pl.ds(pl.multiple_of(h * hdim, hdim), hdim)
            arow = a_rows[pl.ds(h, 1), :]
            cbv = cb[h]
            w0 = (jnp.exp2(jnp.minimum(cbv - arow[:, :half], 126.0)) * masked[:, :half]).astype(BF16)
            w1 = (jnp.exp2(jnp.minimum(cbv[half:] - arow[:, half:], 126.0)) * masked[half:, half:]).astype(BF16)
            fv = conv[:, fcols]
            first = jnp.dot(w0, fv[:half], preferred_element_type=F32)
            second = jnp.dot(w1, fv[half:], preferred_element_type=F32)
            inner = jnp.concatenate([first[:half], first[half:] + second], axis=0)
            gv = gate[:, fcols].astype(F32)
            sg = gv * (1.0 / (1.0 + jnp.exp(-gv)))
            yv[:, fcols] = (inner + skip_smem[h] * fv.astype(F32)) * sg
            tpos = lax.broadcasted_iota(jnp.int32, (rows, hdim), 0)
            lift = jnp.where(offs[...] >= (tpos + 1).astype(F32), jnp.exp2(cbv), 0.0)
            g2[:, fcols] = lift * sg

    def relay(r):
        c = theirs + r
        sl = chunk_cols(c)

        @pl.when(gets_early)
        def _():
            a_copy(r).wait_recv()

        @pl.when((d + 2 < ctx_size) & even)
        def _():
            sout[r] = (arecv[r].astype(F32) + kin[:, sl] * own[c]).astype(BF16)
            s_copy(r).start()

        @pl.when((d + 2 < ctx_size) & odd)
        def _():
            sout[r] = (own[c] + kown[:, sl] * arecv[r].astype(F32)).astype(BF16)
            s_copy(r).start()

    def finish(c, st):
        sl = chunk_cols(c)
        fs = jnp.dot(out_b[...], st, preferred_element_type=F32)
        gt = yv[:, sl] + fs * g2[:, sl]
        gated[:, sl] = gt.astype(gated.dtype)
        squares = gt * gt
        total = squares[:, :hdim]
        for k in range(1, pair):
            total = total + squares[:, k * hdim : (k + 1) * hdim]
        part[...] += total
        out_copy(c).start()

    def pass_on(r):
        c = theirs + r
        sl = chunk_cols(c)

        @pl.when(d >= 2)
        def _():
            s_copy(r).wait_recv()

        @pl.when(even)
        def _():
            lsend[r] = (own[c] + kown[:, sl] * srecv[r].astype(F32)).astype(BF16)
            f_copy(r).start()
            finish(c, srecv[r])

        @pl.when(odd)
        def _():
            @pl.when(d >= 2)
            def _():
                g_copy(r).start()

            finish(c, (arecv[r].astype(F32) + kin[:, sl] * srecv[r].astype(F32)).astype(BF16))

    lag = min(LAG, part_chunks)

    keep_msg.wait_recv()

    def main_body(i, _):
        @pl.when(i < part_chunks)
        def _():
            local_part(2 * i)
            relay(i)
            local_part(2 * i + 1)

        @pl.when(i >= lag)
        def _():
            pass_on(i - lag)

        return 0

    lax.fori_loop(0, part_chunks + lag, main_body, 0)

    def last_body(r, _):
        @pl.when(gets_late)
        def _():
            f_copy(r).wait_recv()

        finish(mine + r, lrecv[r])
        return 0

    lax.fori_loop(0, part_chunks, last_body, 0)

    ones = jnp.ones((8, hdim), F32)
    sq[...] = lax.dot_general(ones, part[...], (((1,), (1,)), ((), ())), precision=EXACT, preferred_element_type=F32)[:1]

    def sq_copy(k):
        return remote(
            sq, sqr.at[k - 1], sqsend.at[k - 1], sqrecv.at[k - 1], (d, lax.rem(hd + k, head_size))
        )

    for k in range(1, head_size):
        sq_copy(k).start()
    total = sq[...]
    for k in range(1, head_size):
        sq_copy(k).wait_recv()
        total = total + sqr[k - 1]
    scale = lax.rsqrt(total / (cols * head_size) + 1e-05)
    scale_ref[...] = scale

    for k in range(1, head_size):
        sq_copy(k).wait_send()

    @pl.when(d + 1 < ctx_size)
    def _():
        halo_p.wait_send()
        halo_f.wait_send()

    keep_msg.wait_send()

    def drain(r, _):
        out_copy(2 * r).wait()
        out_copy(2 * r + 1).wait()

        @pl.when(sends_early)
        def _():
            a_copy(r).wait_send()

        @pl.when(d + 2 < ctx_size)
        def _():
            s_copy(r).wait_send()

        @pl.when(sends_late)
        def _():
            f_copy(r).wait_send()

        return 0

    lax.fori_loop(0, part_chunks, drain, 0)


def short_body(
    feat_in, gate_in, state_proj, step_raw, doc_offset, feat_taps, feat_bias,
    proj_taps, proj_bias, step_bias, decay_log, skip_gain, norm_gain,
):
    heads, rows = step_raw.shape
    cols = feat_in.shape[1]
    hdim = cols // heads
    state = state_proj.shape[1] // 2
    ctx_size = lax.axis_size("ctx")
    head_size = lax.axis_size("head")
    pair = PAIR
    chunks = heads // pair
    width = pair * hdim
    vm = pl.BlockSpec(memory_space=pltpu.VMEM)
    sm = pl.BlockSpec(memory_space=pltpu.SMEM)
    anywhere = pl.BlockSpec(memory_space=pl.ANY)
    hbm = pl.BlockSpec(memory_space=pltpu.HBM)
    V = pltpu.VMEM
    DMA = pltpu.SemaphoreType.DMA
    gated, scale = pl.pallas_call(
        functools.partial(mixer_kernel, ctx_size, head_size, pair),
        out_shape=(
            jax.ShapeDtypeStruct((rows, cols), GATED),
            jax.ShapeDtypeStruct((1, rows), F32),
        ),
        in_specs=[hbm, hbm, hbm, vm, vm, sm, vm, vm, vm, vm, vm, vm, sm],
        out_specs=(anywhere, vm),
        scratch_shapes=[
            V((rows, cols), BF16), V((rows, cols), BF16), V((rows, 2 * state), BF16),
            V((rows + 8, cols), F32), V((rows + 8, 2 * state), F32),
            V((8, cols), BF16), V((8, 2 * state), BF16), V((rows, cols), BF16),
            V((state, rows), F32), V((rows, 2 * state), BF16), V((rows, state), BF16), V((rows, rows), F32),
            V((heads, rows, hdim), F32), V((heads, rows), F32), V((heads, rows), F32),
            V((rows, hdim), F32), V((chunks, state, width), F32),
            V((chunks, state, width), BF16), V((chunks // 2, state, width), BF16),
            V((chunks // 2, state, width), BF16), V((chunks // 2, state, width), BF16),
            V((chunks // 2, state, width), BF16), V((chunks // 2, state, width), BF16),
            V((1, cols), F32), V((1, cols), F32), V((rows, cols), F32), V((rows, cols), F32),
            V((rows, cols), GATED), V((rows, hdim), F32),
            V((1, rows), F32), V((head_size - 1, 1, rows), F32),
            DMA((chunks,)), DMA((chunks,)), DMA((chunks,)), DMA, DMA((2,)), DMA((2,)), DMA((2,)),
            *[DMA((chunks // 2,)) for _ in range(6)],
            DMA((head_size - 1,)), DMA((head_size - 1,)),
        ],
        compiler_params=pltpu.CompilerParams(collective_id=0, has_side_effects=True),
        name="mixer",
    )(
        feat_in, gate_in, state_proj, step_raw, doc_offset[None, :], doc_offset, feat_taps,
        feat_bias[None, :], proj_taps, proj_bias[None, :], step_bias[None, :], decay_log[None, :], skip_gain,
    )
    return (gated.astype(F32) * scale[0][:, None] * norm_gain[None, :]).astype(BF16)


def solution(mesh):
    ctx_size = mesh.shape["ctx"]

    def chosen(*args):
        row_count = args[0].shape[0]
        longest_doc = row_count * ctx_size // 4
        span_back = (longest_doc + row_count - 2) // row_count
        if span_back == 2 and ctx_size % 2 == 0:
            return short_body(*args)
        return body(*args)

    return jax.shard_map(
        chosen,
        mesh=mesh,
        in_specs=(
            P("ctx", "head"),
            P("ctx", "head"),
            P("ctx", None),
            P("head", "ctx"),
            P("ctx"),
            P(None, "head"),
            P("head"),
            P(),
            P(),
            P("head"),
            P("head"),
            P("head"),
            P("head"),
        ),
        out_specs=P("ctx", "head"),
        check_vma=False,
    )
```

profile of v0, /device:TPU:25, one launch (start us, length us, event | category | flops | bytes accessed | tf_op | source)
XLA Modules:
  0.0 27.7 jit_solution(14228385056144826875)
XLA Ops:
  0.0 0.0 copy-start
  0.0 25.1 %mixer.1 = (bf16[256,2048]{1,0:T(8,128)(2,1)}, f32[1,256]{1,0:T(1,128)}) custom-call(bf16[256,2048]{1,0:T(8,128)(2,1)} %feat_hbm.1, bf16[256,2048]{1,0:T(8,128)(2,1)} %gate_hbm.1, bf16[256,256]{1,0:T(8,128)(2,1)} %proj_hbm.1, f32[16,256]{1,0:T(8,128)} %step_ref.1, s32[1,256]{1,0:T(1,128)} %bitcast.7, s32[256]{0:T(256)} %offset_smem.1, f32[4,2048]{1,0:T(4,128)} %taps_ref.1, ...), custom_call_target="tpu_custom_call" | custom-call | tf_op jit(solution)/shard_map/mixer/pallas_call | solution.py:531
  25.1 0.0 copy-done
  25.2 2.5 %multiply_convert_fusion = bf16[256,2048]{1,0:T(8,128)(2,1)} fusion(bf16[256,2048]{1,0:T(8,128)(2,1)} %get-tuple-element.7, f32[2048]{0:T(1024)S(1)} %copy-done, f32[256]{0:T(256)} %bitcast.9), kind=kLoop, calls=%fused_computation | loop fusion | flops 2097152 | bytes 2106368 | tf_op jit(solution)/shard_map/convert_element_type | solution.py:562
Async XLA Ops:
  0.0 25.1 %copy-start = (f32[2048]{0:T(1024)S(1)}, f32[2048]{0:T(1024)}, u32[]{:S(2)}) copy-start(f32[2048]{0:T(1024)} %param.25) | copy-start | bytes 24580
where the time goes:
time: 27.9 us; the launch traced here: 27.7 us
  Pallas kernels  25.1 us (90%)
  other arithmetic  2.5 us (9%)
    pallas_call x1, Pallas kernels, short_body(): pl.pallas_call(functools.partial(mixer_kernel, ctx_size, head_size, pair)...  25.1 us
    convert_element_type x1, other arithmetic, short_body(): (gated.astype(F32) * scale[0][:, None] * norm_gain[None, :]).astype(BF16)  2.5 us

commit v1 on v0

--- a/solution.py
+++ b/solution.py
@@ -476,7 +476,7 @@
         sq_copy(k).wait_recv()
         total = total + sqr[k - 1]
     scale = lax.rsqrt(total / (cols * head_size) + 1e-05)
-    scale_ref[...] = scale
+    scale_ref[...] = jnp.broadcast_to(to_column(scale, rows), scale_ref.shape)
 
     for k in range(1, head_size):
         sq_copy(k).wait_send()
@@ -507,6 +507,45 @@
         return 0
 
     lax.fori_loop(0, part_chunks, drain, 0)
+
+
+STRIPE = 32
+
+
+def scale_kernel(gated_ref, scale_ref, gain_ref, out_hbm, staged, sems):
+    rows, cols = staged.shape
+    lanes = scale_ref.shape[1]
+    stripe = min(STRIPE, rows)
+
+    def out_copy(r):
+        rs = pl.ds(r * stripe, stripe)
+        return pltpu.make_async_copy(staged.at[rs, :], out_hbm.at[rs, :], sems.at[r])
+
+    for r in range(rows // stripe):
+        rs = slice(r * stripe, (r + 1) * stripe)
+        scale = scale_ref[rs, :]
+        for c in range(cols // lanes):
+            cs = slice(c * lanes, (c + 1) * lanes)
+            staged[rs, cs] = (gated_ref[rs, cs].astype(F32) * scale * gain_ref[:, cs]).astype(BF16)
+        out_copy(r).start()
+    for r in range(rows // stripe):
+        out_copy(r).wait()
+
+
+def finish_call(gated, scale, gain):
+    rows, cols = gated.shape
+    vm = pl.BlockSpec(memory_space=pltpu.VMEM)
+    return pl.pallas_call(
+        scale_kernel,
+        out_shape=jax.ShapeDtypeStruct((rows, cols), BF16),
+        in_specs=[vm, vm, vm],
+        out_specs=pl.BlockSpec(memory_space=pltpu.HBM),
+        scratch_shapes=[
+            pltpu.VMEM((rows, cols), BF16), pltpu.SemaphoreType.DMA((rows // min(STRIPE, rows),)),
+        ],
+        compiler_params=pltpu.CompilerParams(vmem_limit_bytes=8 << 20),
+        name="scale",
+    )(gated, scale, gain)
 
 
 def short_body(
@@ -532,7 +571,7 @@
         functools.partial(mixer_kernel, ctx_size, head_size, pair),
         out_shape=(
             jax.ShapeDtypeStruct((rows, cols), GATED),
-            jax.ShapeDtypeStruct((1, rows), F32),
+            jax.ShapeDtypeStruct((rows, hdim), F32),
         ),
         in_specs=[hbm, hbm, hbm, vm, vm, sm, vm, vm, vm, vm, vm, vm, sm],
         out_specs=(anywhere, vm),
@@ -548,18 +587,23 @@
             V((chunks // 2, state, width), BF16), V((chunks // 2, state, width), BF16),
             V((1, cols), F32), V((1, cols), F32), V((rows, cols), F32), V((rows, cols), F32),
             V((rows, cols), GATED), V((rows, hdim), F32),
-            V((1, rows), F32), V((head_size - 1, 1, rows), F32),
+            V((1, rows), F32), V((8, 1, rows), F32),
             DMA((chunks,)), DMA((chunks,)), DMA((chunks,)), DMA, DMA((2,)), DMA((2,)), DMA((2,)),
             *[DMA((chunks // 2,)) for _ in range(6)],
             DMA((head_size - 1,)), DMA((head_size - 1,)),
         ],
-        compiler_params=pltpu.CompilerParams(collective_id=0, has_side_effects=True),
+        compiler_params=pltpu.CompilerParams(
+            collective_id=0, has_side_effects=True, vmem_limit_bytes=40 << 20
+        ),
         name="mixer",
-    )(
-        feat_in, gate_in, state_proj, step_raw, doc_offset[None, :], doc_offset, feat_taps,
-        feat_bias[None, :], proj_taps, proj_bias[None, :], step_bias[None, :], decay_log[None, :], skip_gain,
-    )
-    return (gated.astype(F32) * scale[0][:, None] * norm_gain[None, :]).astype(BF16)
+    )(*[
+        pltpu.with_memory_space_constraint(operand, pltpu.HBM)
+        for operand in (
+            feat_in, gate_in, state_proj, step_raw, doc_offset[None, :], doc_offset, feat_taps,
+            feat_bias[None, :], proj_taps, proj_bias[None, :], step_bias[None, :], decay_log[None, :], skip_gain,
+        )
+    ])
+    return finish_call(gated, scale, norm_gain[None, :])
 
 
 def solution(mesh):

time: 27.9 us -> 26 us (0.932)
  other arithmetic: 2.5 us -> 0 us
  Pallas kernels: 25.1 us -> 25.8 us
    convert_element_type x1 -> x0, other arithmetic: 2.5 us -> none  [short_body(): (gated.astype(F32) * scale[0][:, None] * norm_gain[None, :]).astype(BF16)]
    pallas_call x0 -> x1, Pallas kernels: none -> 1.06 us  [finish_call(): pl.pallas_call(scale_kernel, out_shape=jax.ShapeDtypeStruct((rows, cols),...]
    pallas_call x1, Pallas kernels: 25.1 us -> 24.7 us  [short_body(): pl.pallas_call(functools.partial(mixer_kernel, ctx_size, head_size, pair)...]
where the time goes in v1:
time: 26 us; the launch traced here: 25.8 us
  Pallas kernels  25.8 us (99%)
    pallas_call x1, Pallas kernels, short_body(): pl.pallas_call(functools.partial(mixer_kernel, ctx_size, head_size, pair)...  24.7 us
    pallas_call x1, Pallas kernels, finish_call(): pl.pallas_call(scale_kernel, out_shape=jax.ShapeDtypeStruct((rows, cols),...  1.06 us

profile of v1, /device:TPU:25, one launch (start us, length us, event | category | flops | bytes accessed | tf_op | source)
XLA Modules:
  0.0 25.8 jit_solution(1537221730356548998)
XLA Ops:
  0.0 0.0 copy-start
  0.0 24.7 %mixer.1 = (bf16[256,2048]{1,0:T(8,128)(2,1)S(1)}, f32[256,128]{1,0:T(8,128)S(1)}) custom-call(bf16[256,2048]{1,0:T(8,128)(2,1)} %feat_hbm.1, bf16[256,2048]{1,0:T(8,128)(2,1)} %gate_hbm.1, bf16[256,256]{1,0:T(8,128)(2,1)} %proj_hbm.1, f32[16,256]{1,0:T(8,128)} %step_ref.1, s32[1,256]{1,0:T(1,128)} %bitcast.8, s32[256]{0:T(256)} %offset_smem.1, ...), custom_call_target="tpu_custom_call" | custom-call | tf_op jit(solution)/shard_map/mixer/pallas_call | solution.py:570
  24.7 0.0 copy-done
  24.7 1.1 %scale.1 = bf16[256,2048]{1,0:T(8,128)(2,1)} custom-call(bf16[256,2048]{1,0:T(8,128)(2,1)S(1)} %get-tuple-element.7.gated_ref, f32[256,128]{1,0:T(8,128)S(1)} %get-tuple-element.8.scale_ref, f32[1,2048]{1,0:T(1,128)S(1)} %bitcast.6), custom_call_target="tpu_custom_call" | custom-call | tf_op jit(solution)/shard_map/scale/pallas_call | solution.py:538
Async XLA Ops:
  0.0 24.7 %copy-start = (f32[2048]{0:T(1024)S(1)}, f32[2048]{0:T(1024)}, u32[]{:S(2)}) copy-start(f32[2048]{0:T(1024)} %param.25) | copy-start | bytes 24580

commit v2 on v1

--- a/solution.py
+++ b/solution.py
@@ -134,14 +134,12 @@
 
 
 PAIR = 2
-LAG = 2
-EARLY = 8
-GATED = jnp.bfloat16
+LAG = 4
+STRIPE = 32
 
 LOG2E = 1.4426950408889634
 F32 = jnp.float32
 BF16 = jnp.bfloat16
-EXACT = lax.Precision.HIGHEST
 
 
 def to_column(row, size):
@@ -161,14 +159,26 @@
     return summed * (1.0 / (1.0 + jnp.exp(-summed)))
 
 
+def running_sum(values, upper):
+    first = values.astype(BF16)
+    left = values - first.astype(F32)
+    second = left.astype(BF16)
+    third = (left - second.astype(F32)).astype(BF16)
+    count = values.shape[0]
+    sums = jnp.dot(jnp.concatenate([first, second, third], axis=0), upper, preferred_element_type=F32)
+    return sums[:count] + sums[count : 2 * count] + sums[2 * count :]
+
+
 def mixer_kernel(
     ctx_size, head_size, pair,
-    feat_hbm, gate_hbm, proj_hbm, step_ref, offset_ref, offset_smem, taps_ref, bias_ref,
-    ptaps_ref, pbias_ref, sbias_ref, dlog_ref, skip_smem,
-    gated_hbm, scale_ref,
-    feat, gate, proj, xs, xp, rim, prim, conv, in_t, bc, out_b, masked, cb, a_rows, coef,
-    offs, own, send, arecv, srecv, sout, lsend, lrecv, kown, kin, yv, g2, gated, part, sq, sqr,
-    feat_sems, gate_sems, out_sems, proj_sem, halo_send, halo_recv, keep_sems,
+    feat_hbm, gate_hbm, proj_hbm, step_hbm, offset_hbm, taps_hbm, bias_hbm,
+    ptaps_hbm, pbias_hbm, sbias_hbm, dlog_hbm, skip_hbm,
+    gated, scale_ref,
+    step_ref, offset_ref, taps_ref, bias_ref, ptaps_ref, pbias_ref, sbias_ref, dlog_ref, skip_ref,
+    feat, gate, proj, xs, xp, rim, prim, conv, in_t, bc, out_b, masked, cb, a_rows, coef, coef_top,
+    offs, skips, own, send, arecv, srecv, sout, lsend, lrecv, kown, kmate, kprev,
+    top, tin, ext, xt, yv, g2, part, sq, sqr,
+    small_sems, feat_sems, gate_sems, halo_send, halo_recv, keep_send, keep_recv, top_send, top_recv,
     asend, arecv_sem, ssend, srecv_sem, fsend, lrecv_sem, sqsend, sqrecv,
 ):
     d = lax.axis_index("ctx")
@@ -178,6 +188,7 @@
     hdim = cols // heads
     state = in_t.shape[0]
     taps_n = taps_ref.shape[0]
+    edge = taps_n - 1
     width = pair * hdim
     chunks = heads // pair
     half = rows // 2
@@ -185,14 +196,18 @@
     even = d % 2 == 0
     parity = d % 2
     mate = d + 1 - 2 * parity
-    part_chunks = heads // pair // 2
-    mine = parity * part_chunks
-    theirs = part_chunks - mine
+    part_heads = heads // 2
+    part_chunks = chunks // 2
+    mine = parity * part_heads
+    theirs = part_heads - mine
     sends_early = even | (d + 1 < ctx_size)
     gets_early = odd | (d + 2 < ctx_size)
     sends_late = even | (d >= 2)
     gets_late = odd | (d >= 2)
 
+    def cols_of(h, count):
+        return pl.ds(pl.multiple_of(h * hdim, hdim), count * hdim)
+
     def chunk_cols(c):
         return pl.ds(pl.multiple_of(c * width, width), width)
 
@@ -201,9 +216,6 @@
 
     def gate_copy(c):
         return pltpu.make_async_copy(gate_hbm.at[:, chunk_cols(c)], gate.at[:, chunk_cols(c)], gate_sems.at[c])
-
-    def out_copy(c):
-        return pltpu.make_async_copy(gated.at[:, chunk_cols(c)], gated_hbm.at[:, chunk_cols(c)], out_sems.at[c])
 
     def remote(src, dst, ssem, rsem, where):
         return pltpu.make_async_remote_copy(
@@ -221,150 +233,226 @@
             barrier, inc=1, device_id=(d, lax.rem(hd + k, head_size)), device_id_type=pl.DeviceIdType.MESH
         )
 
-    proj_copy = pltpu.make_async_copy(proj_hbm, proj, proj_sem)
-    proj_copy.start()
+    def ordered(i):
+        return lax.rem(mine // pair + i, chunks)
+
+    small = [
+        pltpu.make_async_copy(src, dst, small_sems.at[n])
+        for n, (src, dst) in enumerate((
+            (offset_hbm, offset_ref), (step_hbm, step_ref), (sbias_hbm, sbias_ref), (dlog_hbm, dlog_ref),
+            (ptaps_hbm, ptaps_ref), (pbias_hbm, pbias_ref), (proj_hbm, proj), (taps_hbm, taps_ref),
+            (bias_hbm, bias_ref), (skip_hbm, skip_ref),
+        ))
+    ]
+    for copy in small:
+        copy.start()
     for c in range(chunks):
-        feat_copy(c).start()
+        feat_copy(ordered(c)).start()
     for c in range(chunks):
         gate_copy(c).start()
 
-    off_col = to_column(offset_ref[...].astype(F32), rows)
-    offs[...] = jnp.broadcast_to(off_col, offs.shape)
+    xs[:8, :] = jnp.zeros((8, cols), F32)
+    xp[:8, :] = jnp.zeros((8, 2 * state), F32)
+    part[...] = jnp.zeros_like(part)
+
+    upper = (
+        lax.broadcasted_iota(jnp.int32, (rows, rows), 0) <= lax.broadcasted_iota(jnp.int32, (rows, rows), 1)
+    ).astype(F32).astype(BF16)
+    for copy in small[:4]:
+        copy.wait()
+    offset_row = offset_ref[...].astype(F32)
+    offs[...] = jnp.broadcast_to(to_column(offset_row, rows), offs.shape)
     step = jax.nn.softplus(step_ref[...] + to_column(sbias_ref[...], heads))
     rate = step * (-jnp.exp(to_column(dlog_ref[...], heads)) * LOG2E)
+    cum = running_sum(rate, upper)
+    shifted = cum - jnp.log(step) * LOG2E
+    a_rows[...] = shifted
+    last = offset_row[:, rows - 1 : rows]
+    place = lax.broadcasted_iota(jnp.int32, (heads, rows), 1)
+    reach = rows - 1 - place
+    weight = jnp.where(last >= reach.astype(F32), jnp.exp2(cum[:, rows - 1 : rows] - shifted), 0.0)
+    coef[...] = jnp.where(place >= edge, weight, 0.0)
+    coef_top[...] = weight[:, :hdim]
+    keep = jnp.where(last >= float(rows), jnp.exp2(cum[:, rows - 1 : rows]), 0.0)
+    kown[...] = jnp.broadcast_to(keep, kown.shape)
+
     near = jnp.minimum(d, 2) + jnp.minimum(ctx_size - 1 - d, 2) + head_size - 1
     pl.semaphore_wait(barrier, near)
     halo_f = remote(feat_hbm.at[pl.ds(rows - 8, 8), :], rim, halo_send.at[0], halo_recv.at[0], (d + 1, hd))
     halo_p = remote(proj_hbm.at[pl.ds(rows - 8, 8), :], prim, halo_send.at[1], halo_recv.at[1], (d + 1, hd))
+    keep_on = remote(kown, kprev, keep_send.at[0], keep_recv.at[0], (d + 1, hd))
+    keep_back = remote(kown, kmate, keep_send.at[1], keep_recv.at[1], (d - 1, hd))
+    top_one = remote(top, tin.at[0], top_send.at[0], top_recv.at[0], (d + 1, hd))
+    top_two = remote(top, tin.at[1], top_send.at[1], top_recv.at[1], (d + 2, hd))
 
     @pl.when(d + 1 < ctx_size)
     def _():
         halo_p.start()
         halo_f.start()
-
-    @pl.when(d == 0)
-    def _():
-        rim[...] = jnp.zeros_like(rim)
-        prim[...] = jnp.zeros_like(prim)
-
-    @pl.when(d < 2)
-    def _():
-        srecv[...] = jnp.zeros_like(srecv)
-
-    @pl.when(d == 0)
-    def _():
-        lrecv[...] = jnp.zeros_like(lrecv)
-
-    upper = (
-        lax.broadcasted_iota(jnp.int32, (rows, rows), 0) <= lax.broadcasted_iota(jnp.int32, (rows, rows), 1)
-    ).astype(F32)
-    cum = jnp.dot(rate, upper, precision=EXACT, preferred_element_type=F32)
-    shifted = cum - jnp.log(step) * LOG2E
-    a_rows[...] = shifted
-    last = offset_smem[rows - 1]
-    place = lax.broadcasted_iota(jnp.int32, (heads, rows), 1)
-    coef[...] = jnp.where(last >= rows - 1 - place, jnp.exp2(cum[:, rows - 1 : rows] - shifted), 0.0)
-    keep = jnp.where(last >= rows, jnp.exp2(cum[:, rows - 1 : rows]), 0.0)
+        keep_on.start()
+
+    @pl.when(odd)
+    def _():
+        keep_back.start()
+
+    def conv_all(c):
+        feat_copy(c).wait()
+        sl = chunk_cols(c)
+        xs[8:, sl] = feat[:, sl].astype(F32)
+        conv[:, sl] = tap_sum(
+            lambda lag: xs[8 - lag : 8 + rows - lag, sl], taps_ref[:, sl], bias_ref[:, sl], offs[:, :1], taps_n
+        ).astype(BF16)
+
+    def a_copy(r):
+        return remote(send.at[r], arecv.at[r], asend.at[r], arecv_sem.at[r], (mate, hd))
+
+    def s_copy(r):
+        return remote(sout.at[r], srecv.at[r], ssend.at[r], srecv_sem.at[r], (d + 2, hd))
+
+    def f_copy(r):
+        return remote(lsend.at[r], lrecv.at[r], fsend.at[r], lrecv_sem.at[r], (mate, hd))
+
+    def g_copy(r):
+        return remote(srecv.at[r], lrecv.at[r], fsend.at[r], lrecv_sem.at[r], (mate, hd))
+
+    def contrib(h):
+        scaled = (in_t[...] * coef[pl.ds(h, 1), :]).astype(BF16)
+        return jnp.dot(scaled, conv[:, cols_of(h, 1)], preferred_element_type=F32)
+
+    def mine_body(i, _):
+        conv_all(mine // pair + i)
+        for k in range(pair):
+            r = i * pair + k
+            send[r] = contrib(mine + r).astype(BF16)
+
+            @pl.when(sends_early)
+            def _():
+                a_copy(r).start()
+
+        return 0
+
+    def theirs_body(i, _):
+        conv_all(theirs // pair + i)
+        for k in range(pair):
+            r = i * pair + k
+            own[r] = contrib(theirs + r)
+        return 0
+
+    for copy in small[4:]:
+        copy.wait()
+    xp[8:, :] = proj[...].astype(F32)
+    bc[...] = tap_sum(
+        lambda lag: xp[8 - lag : 8 + rows - lag, :], ptaps_ref[...], pbias_ref[...], offs[:, :1], taps_n
+    ).astype(BF16)
+    in_t[...] = bc[:, :state].astype(F32).T
+    lax.fori_loop(0, part_chunks, mine_body, 0)
+
     cum_t = cum.T
     for h in range(heads):
         cb[h] = jnp.broadcast_to(cum_t[:, h : h + 1], (rows, hdim))
-        kown[:, h * hdim : (h + 1) * hdim] = jnp.broadcast_to(keep[h : h + 1, :], (1, hdim))
-
-    keep_msg = remote(kown, kin, keep_sems.at[0], keep_sems.at[1], (mate, hd))
-    keep_msg.start()
-
-    def conv_main(c):
-        feat_copy(c).wait()
-        sl = chunk_cols(c)
-        xs[8:, sl] = feat[:, sl].astype(F32)
-        conv[16:, sl] = tap_sum(
-            lambda lag: xs[24 - lag : 8 + rows - lag, sl], taps_ref[:, sl], bias_ref[:, sl], offs[16:, :1], taps_n
-        ).astype(BF16)
-
-    def conv_top(c):
-        sl = chunk_cols(c)
+    skips[...] = jnp.broadcast_to(to_column(skip_ref[...], heads), skips.shape)
+
+    @pl.when(d == 0)
+    def _():
+        rim[...] = jnp.zeros_like(rim)
+        prim[...] = jnp.zeros_like(prim)
+        lrecv[...] = jnp.zeros_like(lrecv)
+        kprev[...] = jnp.zeros_like(kprev)
+        tin[0] = jnp.zeros(tin.shape[1:], BF16)
+
+    @pl.when(d < 2)
+    def _():
+        srecv[...] = jnp.zeros_like(srecv)
+        tin[1] = jnp.zeros(tin.shape[1:], BF16)
+
+    lax.fori_loop(0, part_chunks, theirs_body, 0)
+
+    @pl.when(d > 0)
+    def _():
+        keep_on.wait_recv()
+
+    @pl.when(even)
+    def _():
+        keep_back.wait_recv()
+
+    def relay(r):
+        h = theirs + r
+
+        @pl.when(gets_early)
+        def _():
+            a_copy(r).wait_recv()
+
+        @pl.when((d + 2 < ctx_size) & even)
+        def _():
+            sout[r] = (arecv[r].astype(F32) + kmate[pl.ds(h, 1), :] * own[r]).astype(BF16)
+            s_copy(r).start()
+
+        @pl.when((d + 2 < ctx_size) & odd)
+        def _():
+            sout[r] = (own[r] + kown[pl.ds(h, 1), :] * arecv[r].astype(F32)).astype(BF16)
+            s_copy(r).start()
+
+    def pass_on(r):
+        @pl.when(d >= 2)
+        def _():
+            s_copy(r).wait_recv()
+
+        @pl.when(even)
+        def _():
+            lsend[r] = (own[r] + kown[pl.ds(theirs + r, 1), :] * srecv[r].astype(F32)).astype(BF16)
+            f_copy(r).start()
+
+        @pl.when(odd & (d >= 2))
+        def _():
+            g_copy(r).start()
+
+    @pl.when(d > 0)
+    def _():
+        halo_p.wait_recv()
+        halo_f.wait_recv()
+
+    xp[:8, :] = prim[...].astype(F32)
+    bc[:16, :] = tap_sum(
+        lambda lag: xp[8 - lag : 24 - lag, :], ptaps_ref[...], pbias_ref[...], offs[:16, :1], taps_n
+    ).astype(BF16)
+    for c in range(cols // 512):
+        sl = slice(c * 512, (c + 1) * 512)
         xs[:8, sl] = rim[:, sl].astype(F32)
         conv[:16, sl] = tap_sum(
             lambda lag: xs[8 - lag : 24 - lag, sl], taps_ref[:, sl], bias_ref[:, sl], offs[:16, :1], taps_n
         ).astype(BF16)
-
-    def ordered(i):
-        return lax.rem(mine + i, chunks)
-
-    def early_body(c, _):
-        conv_main(ordered(c))
-        return 0
-
-    proj_copy.wait()
-    xp[8:, :] = proj[...].astype(F32)
-    cp = tap_sum(
-        lambda lag: xp[24 - lag : 8 + rows - lag, :], ptaps_ref[...], pbias_ref[...], offs[16:, :1], taps_n
-    ).astype(BF16)
-    bc[16:, :] = cp
-    lax.fori_loop(0, min(EARLY // pair, chunks), early_body, 0)
-
-    @pl.when(d > 0)
-    def _():
-        halo_p.wait_recv()
-        halo_f.wait_recv()
-
-    xp[:8, :] = prim[...].astype(F32)
-    bc[:16, :] = tap_sum(
-        lambda lag: xp[8 - lag : 24 - lag, :], ptaps_ref[...], pbias_ref[...], offs[:16, :1], taps_n
-    ).astype(BF16)
+    weight_t = coef_top[...].T[:8, :]
+    row_id = lax.broadcasted_iota(jnp.int32, weight_t.shape, 0)
+    weight_t = jnp.where(row_id < edge, weight_t, 0.0)
+    in_top = bc[:8, :state].astype(F32)
+    top[:, :state] = jnp.concatenate([in_top[:4], in_top[:4]], axis=0).astype(BF16)
+    for r in range(part_heads):
+        rows_of = [
+            (conv[:8, h * hdim : (h + 1) * hdim].astype(F32) * weight_t[:, h : h + 1])[:4] for h in (r, part_heads + r)
+        ]
+        top[:, state + r * hdim : state + (r + 1) * hdim] = jnp.concatenate(rows_of, axis=0).astype(BF16)
+
+    @pl.when(d + 1 < ctx_size)
+    def _():
+        top_one.start()
+
+    @pl.when(d + 2 < ctx_size)
+    def _():
+        top_two.start()
+
     in_b = bc[:, :state]
-    in_t[...] = in_b.astype(F32).T
     out_b[...] = bc[:, state:]
-
-    def contrib(c):
-        conv_top(c)
-        for k in range(pair):
-            h = c * pair + k
-            scaled = (in_t[...] * coef[pl.ds(h, 1), :]).astype(BF16)
-            fcols = pl.ds(pl.multiple_of(h * hdim, hdim), hdim)
-            got = jnp.dot(scaled, conv[:, fcols], preferred_element_type=F32)
-            own[c, :, k * hdim : (k + 1) * hdim] = got
-            send[c, :, k * hdim : (k + 1) * hdim] = got.astype(BF16)
-
-        @pl.when(sends_early & (c >= mine) & (c < mine + part_chunks))
-        def _():
-            a_copy(c - mine).start()
-
-    def contrib_body(i, _):
-        contrib(ordered(i))
-        return 0
-
-    def late_body(i, _):
-        conv_main(ordered(i))
-        contrib(ordered(i))
-        return 0
-
-    def a_copy(r):
-        return remote(send.at[mine + r], arecv.at[r], asend.at[r], arecv_sem.at[r], (mate, hd))
-
-    def s_copy(r):
-        return remote(sout.at[r], srecv.at[r], ssend.at[r], srecv_sem.at[r], (d + 2, hd))
-
-    def f_copy(r):
-        return remote(lsend.at[r], lrecv.at[r], fsend.at[r], lrecv_sem.at[r], (mate, hd))
-
-    def g_copy(r):
-        return remote(srecv.at[r], lrecv.at[r], fsend.at[r], lrecv_sem.at[r], (mate, hd))
-
-    lax.fori_loop(0, min(EARLY // pair, chunks), contrib_body, 0)
-    lax.fori_loop(min(EARLY // pair, chunks), chunks, late_body, 0)
     scores = lax.dot_general(out_b[...], in_b, (((1,), (1,)), ((), ())), preferred_element_type=F32)
     ti = lax.broadcasted_iota(jnp.int32, (rows, rows), 0)
     si = lax.broadcasted_iota(jnp.int32, (rows, rows), 1)
     gap = ti - si
     masked[...] = jnp.where((gap >= 0) & (offs[:, :1] >= gap.astype(F32)), scores, 0.0)
-    part[...] = jnp.zeros_like(part)
 
     def local_part(c):
         gate_copy(c).wait()
         for k in range(pair):
             h = c * pair + k
-            fcols = pl.ds(pl.multiple_of(h * hdim, hdim), hdim)
+            fcols = cols_of(h, 1)
             arow = a_rows[pl.ds(h, 1), :]
             cbv = cb[h]
             w0 = (jnp.exp2(jnp.minimum(cbv - arow[:, :half], 126.0)) * masked[:, :half]).astype(BF16)
@@ -375,32 +463,37 @@
             inner = jnp.concatenate([first[:half], first[half:] + second], axis=0)
             gv = gate[:, fcols].astype(F32)
             sg = gv * (1.0 / (1.0 + jnp.exp(-gv)))
-            yv[:, fcols] = (inner + skip_smem[h] * fv.astype(F32)) * sg
+            yv[:, fcols] = (inner + skips[pl.ds(h, 1), :] * fv.astype(F32)) * sg
             tpos = lax.broadcasted_iota(jnp.int32, (rows, hdim), 0)
             lift = jnp.where(offs[...] >= (tpos + 1).astype(F32), jnp.exp2(cbv), 0.0)
             g2[:, fcols] = lift * sg
 
-    def relay(r):
-        c = theirs + r
-        sl = chunk_cols(c)
-
-        @pl.when(gets_early)
-        def _():
-            a_copy(r).wait_recv()
-
-        @pl.when((d + 2 < ctx_size) & even)
-        def _():
-            sout[r] = (arecv[r].astype(F32) + kin[:, sl] * own[c]).astype(BF16)
-            s_copy(r).start()
-
-        @pl.when((d + 2 < ctx_size) & odd)
-        def _():
-            sout[r] = (own[c] + kown[:, sl] * arecv[r].astype(F32)).astype(BF16)
-            s_copy(r).start()
-
-    def finish(c, st):
-        sl = chunk_cols(c)
+    def early_terms():
+        @pl.when(d > 0)
+        def _():
+            top_one.wait_recv()
+
+        @pl.when(d > 1)
+        def _():
+            top_two.wait_recv()
+
+        firsts = jnp.concatenate([tin[0, :, :state], tin[1, :, :state]], axis=0)
+        marks = lax.dot_general(out_b[...], firsts, (((1,), (1,)), ((), ())), preferred_element_type=F32)
+        lane = lax.broadcasted_iota(jnp.int32, marks.shape, 1) % 8
+        ext[0] = jnp.where(lane < 4, marks, 0.0).astype(BF16)
+        ext[1] = jnp.where(lane < 4, 0.0, marks).astype(BF16)
+        near_rows = lax.broadcasted_iota(jnp.int32, (8, hdim), 0)
+        for r in range(part_heads):
+            cs = slice(state + r * hdim, state + (r + 1) * hdim)
+            decay = jnp.where(near_rows < 4, kprev[r : r + 1, :], kprev[part_heads + r : part_heads + r + 1, :])
+            xt[:, r * hdim : (r + 1) * hdim] = jnp.concatenate(
+                [tin[0, :, cs].astype(F32), tin[1, :, cs].astype(F32) * decay], axis=0
+            ).astype(BF16)
+
+    def finish(side, r, st):
+        sl = cols_of(side * part_heads + r, pair)
         fs = jnp.dot(out_b[...], st, preferred_element_type=F32)
+        fs = fs + jnp.dot(ext[side], xt[:, cols_of(r, pair)], preferred_element_type=F32)
         gt = yv[:, sl] + fs * g2[:, sl]
         gated[:, sl] = gt.astype(gated.dtype)
         squares = gt * gt
@@ -408,61 +501,59 @@
         for k in range(1, pair):
             total = total + squares[:, k * hdim : (k + 1) * hdim]
         part[...] += total
-        out_copy(c).start()
-
-    def pass_on(r):
-        c = theirs + r
-        sl = chunk_cols(c)
-
-        @pl.when(d >= 2)
-        def _():
-            s_copy(r).wait_recv()
-
+
+    def finish_theirs(r):
         @pl.when(even)
         def _():
-            lsend[r] = (own[c] + kown[:, sl] * srecv[r].astype(F32)).astype(BF16)
-            f_copy(r).start()
-            finish(c, srecv[r])
+            finish(1, r, jnp.concatenate([srecv[r + k] for k in range(pair)], axis=1))
 
         @pl.when(odd)
         def _():
-            @pl.when(d >= 2)
-            def _():
-                g_copy(r).start()
-
-            finish(c, (arecv[r].astype(F32) + kin[:, sl] * srecv[r].astype(F32)).astype(BF16))
-
-    lag = min(LAG, part_chunks)
-
-    keep_msg.wait_recv()
-
-    def main_body(i, _):
-        @pl.when(i < part_chunks)
-        def _():
-            local_part(2 * i)
-            relay(i)
-            local_part(2 * i + 1)
-
-        @pl.when(i >= lag)
-        def _():
-            pass_on(i - lag)
-
+            finish(0, r, jnp.concatenate([
+                (arecv[r + k].astype(F32) + kprev[pl.ds(r + k, 1), :] * srecv[r + k].astype(F32)).astype(BF16)
+                for k in range(pair)
+            ], axis=1))
+
+    lag = min(LAG, part_heads)
+
+    def first_body(i, _):
+        relay(i)
+        local_part(i)
         return 0
 
-    lax.fori_loop(0, part_chunks + lag, main_body, 0)
-
-    def last_body(r, _):
+    def second_body(i, _):
+        relay(i)
+        local_part(i)
+        pass_on(i - lag)
+        return 0
+
+    lax.fori_loop(0, lag, first_body, 0)
+    lax.fori_loop(lag, part_heads, second_body, 0)
+    early_terms()
+    done = 0
+    for r in range(part_heads - lag, part_heads):
+        pass_on(r)
+        if done + pair <= r + 1:
+            finish_theirs(done)
+            done += pair
+    while done < part_heads:
+        finish_theirs(done)
+        done += pair
+
+    def last_body(j, _):
+        r = j * pair
+
         @pl.when(gets_late)
         def _():
-            f_copy(r).wait_recv()
-
-        finish(mine + r, lrecv[r])
+            for k in range(pair):
+                f_copy(r + k).wait_recv()
+
+        finish(parity, r, jnp.concatenate([lrecv[r + k] for k in range(pair)], axis=1))
         return 0
 
     lax.fori_loop(0, part_chunks, last_body, 0)
 
-    ones = jnp.ones((8, hdim), F32)
-    sq[...] = lax.dot_general(ones, part[...], (((1,), (1,)), ((), ())), precision=EXACT, preferred_element_type=F32)[:1]
+    sq[...] = jnp.sum(part[...].T, axis=0, keepdims=True)
 
     def sq_copy(k):
         return remote(
@@ -471,45 +562,46 @@
 
     for k in range(1, head_size):
         sq_copy(k).start()
+
+    @pl.when(d + 1 < ctx_size)
+    def _():
+        halo_p.wait_send()
+        halo_f.wait_send()
+        keep_on.wait_send()
+        top_one.wait_send()
+
+    @pl.when(d + 2 < ctx_size)
+    def _():
+        top_two.wait_send()
+
+    @pl.when(odd)
+    def _():
+        keep_back.wait_send()
+
+    def drain(r, _):
+        @pl.when(sends_early)
+        def _():
+            a_copy(r).wait_send()
+
+        @pl.when(d + 2 < ctx_size)
+        def _():
+            s_copy(r).wait_send()
+
+        @pl.when(sends_late)
+        def _():
+            f_copy(r).wait_send()
+
+        return 0
+
+    lax.fori_loop(0, part_heads, drain, 0)
     total = sq[...]
     for k in range(1, head_size):
         sq_copy(k).wait_recv()
         total = total + sqr[k - 1]
     scale = lax.rsqrt(total / (cols * head_size) + 1e-05)
-    scale_ref[...] = jnp.broadcast_to(to_column(scale, rows), scale_ref.shape)
-
+    scale_ref[...] = jnp.broadcast_to(scale, (hdim, rows)).T
     for k in range(1, head_size):
         sq_copy(k).wait_send()
-
-    @pl.when(d + 1 < ctx_size)
-    def _():
-        halo_p.wait_send()
-        halo_f.wait_send()
-
-    keep_msg.wait_send()
-
-    def drain(r, _):
-        out_copy(2 * r).wait()
-        out_copy(2 * r + 1).wait()
-
-        @pl.when(sends_early)
-        def _():
-            a_copy(r).wait_send()
-
-        @pl.when(d + 2 < ctx_size)
-        def _():
-            s_copy(r).wait_send()
-
-        @pl.when(sends_late)
-        def _():
-            f_copy(r).wait_send()
-
-        return 0
-
-    lax.fori_loop(0, part_chunks, drain, 0)
-
-
-STRIPE = 32
 
 
 def scale_kernel(gated_ref, scale_ref, gain_ref, out_hbm, staged, sems):
@@ -556,53 +648,53 @@
     cols = feat_in.shape[1]
     hdim = cols // heads
     state = state_proj.shape[1] // 2
+    taps = feat_taps.shape[0]
     ctx_size = lax.axis_size("ctx")
     head_size = lax.axis_size("head")
     pair = PAIR
     chunks = heads // pair
-    width = pair * hdim
+    some = heads // 2
     vm = pl.BlockSpec(memory_space=pltpu.VMEM)
-    sm = pl.BlockSpec(memory_space=pltpu.SMEM)
-    anywhere = pl.BlockSpec(memory_space=pl.ANY)
     hbm = pl.BlockSpec(memory_space=pltpu.HBM)
     V = pltpu.VMEM
     DMA = pltpu.SemaphoreType.DMA
+    piece = (some, state, hdim)
+    operands = (
+        feat_in, gate_in, state_proj, step_raw, doc_offset[None, :], feat_taps,
+        feat_bias[None, :], proj_taps, proj_bias[None, :], step_bias[None, :], decay_log[None, :], skip_gain[None, :],
+    )
     gated, scale = pl.pallas_call(
         functools.partial(mixer_kernel, ctx_size, head_size, pair),
         out_shape=(
-            jax.ShapeDtypeStruct((rows, cols), GATED),
+            jax.ShapeDtypeStruct((rows, cols), BF16),
             jax.ShapeDtypeStruct((rows, hdim), F32),
         ),
-        in_specs=[hbm, hbm, hbm, vm, vm, sm, vm, vm, vm, vm, vm, vm, sm],
-        out_specs=(anywhere, vm),
+        in_specs=[hbm] * len(operands),
+        out_specs=(vm, vm),
         scratch_shapes=[
+            V((heads, rows), F32), V((1, rows), jnp.int32), V((taps, cols), F32), V((1, cols), F32),
+            V((taps, 2 * state), F32), V((1, 2 * state), F32), V((1, heads), F32), V((1, heads), F32),
+            V((1, heads), F32),
             V((rows, cols), BF16), V((rows, cols), BF16), V((rows, 2 * state), BF16),
             V((rows + 8, cols), F32), V((rows + 8, 2 * state), F32),
             V((8, cols), BF16), V((8, 2 * state), BF16), V((rows, cols), BF16),
             V((state, rows), F32), V((rows, 2 * state), BF16), V((rows, state), BF16), V((rows, rows), F32),
-            V((heads, rows, hdim), F32), V((heads, rows), F32), V((heads, rows), F32),
-            V((rows, hdim), F32), V((chunks, state, width), F32),
-            V((chunks, state, width), BF16), V((chunks // 2, state, width), BF16),
-            V((chunks // 2, state, width), BF16), V((chunks // 2, state, width), BF16),
-            V((chunks // 2, state, width), BF16), V((chunks // 2, state, width), BF16),
-            V((1, cols), F32), V((1, cols), F32), V((rows, cols), F32), V((rows, cols), F32),
-            V((rows, cols), GATED), V((rows, hdim), F32),
-            V((1, rows), F32), V((8, 1, rows), F32),
-            DMA((chunks,)), DMA((chunks,)), DMA((chunks,)), DMA, DMA((2,)), DMA((2,)), DMA((2,)),
-            *[DMA((chunks // 2,)) for _ in range(6)],
+            V((heads, rows, hdim), F32), V((heads, rows), F32), V((heads, rows), F32), V((heads, hdim), F32),
+            V((rows, hdim), F32), V((heads, hdim), F32),
+            V(piece, F32), V(piece, BF16), V(piece, BF16), V(piece, BF16), V(piece, BF16), V(piece, BF16),
+            V(piece, BF16),
+            V((heads, hdim), F32), V((heads, hdim), F32), V((heads, hdim), F32),
+            V((8, state + cols // 2), BF16), V((2, 8, state + cols // 2), BF16), V((2, rows, 16), BF16),
+            V((16, cols // 2), BF16),
+            V((rows, cols), F32), V((rows, cols), F32), V((rows, hdim), F32),
+            V((1, rows), F32), V((head_size - 1, 1, rows), F32),
+            DMA((10,)), DMA((chunks,)), DMA((chunks,)), *[DMA((2,)) for _ in range(6)],
+            *[DMA((some,)) for _ in range(6)],
             DMA((head_size - 1,)), DMA((head_size - 1,)),
         ],
-        compiler_params=pltpu.CompilerParams(
-            collective_id=0, has_side_effects=True, vmem_limit_bytes=40 << 20
-        ),
+        compiler_params=pltpu.CompilerParams(collective_id=0, has_side_effects=True, vmem_limit_bytes=40 << 20),
         name="mixer",
-    )(*[
-        pltpu.with_memory_space_constraint(operand, pltpu.HBM)
-        for operand in (
-            feat_in, gate_in, state_proj, step_raw, doc_offset[None, :], doc_offset, feat_taps,
-            feat_bias[None, :], proj_taps, proj_bias[None, :], step_bias[None, :], decay_log[None, :], skip_gain,
-        )
-    ])
+    )(*[pltpu.with_memory_space_constraint(operand, pltpu.HBM) for operand in operands])
     return finish_call(gated, scale, norm_gain[None, :])
 
 

time: 26 us -> 24 us (0.923)
  the two profiles are of different devices: /device:TPU:25 before, /device:TPU:9 now
where the time goes in v2:
time: 24 us; the launch traced here: 23.8 us
  Pallas kernels  23.8 us (99%)
    pallas_call x1, Pallas kernels, short_body(): pl.pallas_call(functools.partial(mixer_kernel, ctx_size, head_size, pair)...  22.8 us
    pallas_call x1, Pallas kernels, finish_call(): pl.pallas_call(scale_kernel, out_shape=jax.ShapeDtypeStruct((rows, cols),...  1.06 us

profile of v2, /device:TPU:9, one launch (start us, length us, event | category | flops | bytes accessed | tf_op | source)
XLA Modules:
  0.0 23.8 jit_solution(9008036043121721690)
XLA Ops:
  0.0 0.0 copy-start
  0.0 22.8 %mixer.1 = (bf16[256,2048]{1,0:T(8,128)(2,1)S(1)}, f32[256,128]{1,0:T(8,128)S(1)}) custom-call(bf16[256,2048]{1,0:T(8,128)(2,1)} %feat_hbm.1, bf16[256,2048]{1,0:T(8,128)(2,1)} %gate_hbm.1, bf16[256,256]{1,0:T(8,128)(2,1)} %proj_hbm.1, f32[16,256]{1,0:T(8,128)} %step_hbm.1, s32[1,256]{1,0:T(1,128)} %bitcast.9, f32[4,2048]{1,0:T(4,128)} %taps_hbm.1, ...), custom_call_target="tpu_custom_call" | custom-call | tf_op jit(solution)/shard_map/mixer/pallas_call | solution.py:666
  22.8 0.0 copy-done
  22.8 1.1 %scale.1 = bf16[256,2048]{1,0:T(8,128)(2,1)} custom-call(bf16[256,2048]{1,0:T(8,128)(2,1)S(1)} %get-tuple-element.7.gated_ref, f32[256,128]{1,0:T(8,128)S(1)} %get-tuple-element.8.scale_ref, f32[1,2048]{1,0:T(1,128)S(1)} %bitcast.7), custom_call_target="tpu_custom_call" | custom-call | tf_op jit(solution)/shard_map/scale/pallas_call | solution.py:630
Async XLA Ops:
  0.0 22.8 %copy-start = (f32[2048]{0:T(1024)S(1)}, f32[2048]{0:T(1024)}, u32[]{:S(2)}) copy-start(f32[2048]{0:T(1024)} %param.25) | copy-start | bytes 24580

commit v3 on v2

--- a/solution.py
+++ b/solution.py
@@ -134,7 +134,8 @@
 
 
 PAIR = 2
-LAG = 4
+READY = 2
+LAG = 5
 STRIPE = 32
 
 LOG2E = 1.4426950408889634
@@ -175,10 +176,10 @@
     ptaps_hbm, pbias_hbm, sbias_hbm, dlog_hbm, skip_hbm,
     gated, scale_ref,
     step_ref, offset_ref, taps_ref, bias_ref, ptaps_ref, pbias_ref, sbias_ref, dlog_ref, skip_ref,
-    feat, gate, proj, xs, xp, rim, prim, conv, in_t, bc, out_b, masked, cb, a_rows, coef, coef_top,
+    feat, gate, proj, xs, xp, rim, conv, in_t, bc, out_b, masked, cb, a_rows, coef, coef_top,
     offs, skips, own, send, arecv, srecv, sout, lsend, lrecv, kown, kmate, kprev,
-    top, tin, ext, xt, yv, g2, part, sq, sqr,
-    small_sems, feat_sems, gate_sems, halo_send, halo_recv, keep_send, keep_recv, top_send, top_recv,
+    top, tin, ext, xt, yv, g2, part, sq, sqr, tail, tail_proj, tail_half, tail_sems,
+    small_sems, feat_sems, gate_sem, halo_send, halo_recv, keep_send, keep_recv, top_send, top_recv,
     asend, arecv_sem, ssend, srecv_sem, fsend, lrecv_sem, sqsend, sqrecv,
 ):
     d = lax.axis_index("ctx")
@@ -214,8 +215,7 @@
     def feat_copy(c):
         return pltpu.make_async_copy(feat_hbm.at[:, chunk_cols(c)], feat.at[:, chunk_cols(c)], feat_sems.at[c])
 
-    def gate_copy(c):
-        return pltpu.make_async_copy(gate_hbm.at[:, chunk_cols(c)], gate.at[:, chunk_cols(c)], gate_sems.at[c])
+    gate_copy = pltpu.make_async_copy(gate_hbm, gate, gate_sem)
 
     def remote(src, dst, ssem, rsem, where):
         return pltpu.make_async_remote_copy(
@@ -236,6 +236,12 @@
     def ordered(i):
         return lax.rem(mine // pair + i, chunks)
 
+    tail_copies = [
+        pltpu.make_async_copy(feat_hbm.at[pl.ds(rows - 8, 8), :], tail, tail_sems.at[0]),
+        pltpu.make_async_copy(proj_hbm.at[pl.ds(rows - 8, 8), :], tail_proj, tail_sems.at[1]),
+    ]
+    for copy in tail_copies:
+        copy.start()
     small = [
         pltpu.make_async_copy(src, dst, small_sems.at[n])
         for n, (src, dst) in enumerate((
@@ -248,8 +254,7 @@
         copy.start()
     for c in range(chunks):
         feat_copy(ordered(c)).start()
-    for c in range(chunks):
-        gate_copy(c).start()
+    gate_copy.start()
 
     xs[:8, :] = jnp.zeros((8, cols), F32)
     xp[:8, :] = jnp.zeros((8, 2 * state), F32)
@@ -276,10 +281,15 @@
     keep = jnp.where(last >= float(rows), jnp.exp2(cum[:, rows - 1 : rows]), 0.0)
     kown[...] = jnp.broadcast_to(keep, kown.shape)
 
+    for copy in tail_copies:
+        copy.wait()
+    tail_half[:, cols // 2 :] = tail_proj[...]
+    tail_half[:, : cols // 2] = jnp.concatenate(
+        [tail[:, : cols // 2].astype(F32)[4:], tail[:, cols // 2 :].astype(F32)[4:]], axis=0
+    ).astype(BF16)
     near = jnp.minimum(d, 2) + jnp.minimum(ctx_size - 1 - d, 2) + head_size - 1
     pl.semaphore_wait(barrier, near)
-    halo_f = remote(feat_hbm.at[pl.ds(rows - 8, 8), :], rim, halo_send.at[0], halo_recv.at[0], (d + 1, hd))
-    halo_p = remote(proj_hbm.at[pl.ds(rows - 8, 8), :], prim, halo_send.at[1], halo_recv.at[1], (d + 1, hd))
+    halo = remote(tail_half, rim, halo_send, halo_recv, (d + 1, hd))
     keep_on = remote(kown, kprev, keep_send.at[0], keep_recv.at[0], (d + 1, hd))
     keep_back = remote(kown, kmate, keep_send.at[1], keep_recv.at[1], (d - 1, hd))
     top_one = remote(top, tin.at[0], top_send.at[0], top_recv.at[0], (d + 1, hd))
@@ -287,8 +297,7 @@
 
     @pl.when(d + 1 < ctx_size)
     def _():
-        halo_p.start()
-        halo_f.start()
+        halo.start()
         keep_on.start()
 
     @pl.when(odd)
@@ -304,16 +313,16 @@
         ).astype(BF16)
 
     def a_copy(r):
-        return remote(send.at[r], arecv.at[r], asend.at[r], arecv_sem.at[r], (mate, hd))
+        return remote(send.at[r], arecv.at[r], asend, arecv_sem.at[r], (mate, hd))
 
     def s_copy(r):
-        return remote(sout.at[r], srecv.at[r], ssend.at[r], srecv_sem.at[r], (d + 2, hd))
+        return remote(sout.at[r], srecv.at[r], ssend, srecv_sem.at[r], (d + 2, hd))
 
     def f_copy(r):
-        return remote(lsend.at[r], lrecv.at[r], fsend.at[r], lrecv_sem.at[r], (mate, hd))
+        return remote(lsend.at[r], lrecv.at[r], fsend, lrecv_sem.at[r // pair], (mate, hd))
 
     def g_copy(r):
-        return remote(srecv.at[r], lrecv.at[r], fsend.at[r], lrecv_sem.at[r], (mate, hd))
+        return remote(srecv.at[r], lrecv.at[r], fsend, lrecv_sem.at[r // pair], (mate, hd))
 
     def contrib(h):
         scaled = (in_t[...] * coef[pl.ds(h, 1), :]).astype(BF16)
@@ -347,77 +356,80 @@
     in_t[...] = bc[:, :state].astype(F32).T
     lax.fori_loop(0, part_chunks, mine_body, 0)
 
+    @pl.when(d == 0)
+    def _():
+        rim[...] = jnp.zeros_like(rim)
+        lrecv[...] = jnp.zeros_like(lrecv)
+        kprev[...] = jnp.zeros_like(kprev)
+        tin[0] = jnp.zeros(tin.shape[1:], BF16)
+
+    @pl.when(d < 2)
+    def _():
+        srecv[...] = jnp.zeros_like(srecv)
+        tin[1] = jnp.zeros(tin.shape[1:], BF16)
+
+    lax.fori_loop(0, part_chunks, theirs_body, 0)
+
+    @pl.when(d > 0)
+    def _():
+        keep_on.wait_recv()
+
+    @pl.when(even)
+    def _():
+        keep_back.wait_recv()
+
+    def relay(r):
+        h = theirs + r
+
+        @pl.when(gets_early)
+        def _():
+            a_copy(r).wait_recv()
+
+        @pl.when((d + 2 < ctx_size) & even)
+        def _():
+            sout[r] = (arecv[r].astype(F32) + kmate[pl.ds(h, 1), :] * own[r]).astype(BF16)
+            s_copy(r).start()
+
+        @pl.when((d + 2 < ctx_size) & odd)
+        def _():
+            sout[r] = (own[r] + kown[pl.ds(h, 1), :] * arecv[r].astype(F32)).astype(BF16)
+            s_copy(r).start()
+
+    def pass_on(r):
+        @pl.when(d >= 2)
+        def _():
+            s_copy(r).wait_recv()
+
+        @pl.when(even)
+        def _():
+            lsend[r] = (own[r] + kown[pl.ds(theirs + r, 1), :] * srecv[r].astype(F32)).astype(BF16)
+            f_copy(r).start()
+
+        @pl.when(odd & (d >= 2))
+        def _():
+            g_copy(r).start()
+
+    ready = min(READY, part_heads)
+    for r in range(ready):
+        relay(r)
     cum_t = cum.T
     for h in range(heads):
         cb[h] = jnp.broadcast_to(cum_t[:, h : h + 1], (rows, hdim))
     skips[...] = jnp.broadcast_to(to_column(skip_ref[...], heads), skips.shape)
 
-    @pl.when(d == 0)
-    def _():
-        rim[...] = jnp.zeros_like(rim)
-        prim[...] = jnp.zeros_like(prim)
-        lrecv[...] = jnp.zeros_like(lrecv)
-        kprev[...] = jnp.zeros_like(kprev)
-        tin[0] = jnp.zeros(tin.shape[1:], BF16)
-
-    @pl.when(d < 2)
-    def _():
-        srecv[...] = jnp.zeros_like(srecv)
-        tin[1] = jnp.zeros(tin.shape[1:], BF16)
-
-    lax.fori_loop(0, part_chunks, theirs_body, 0)
-
     @pl.when(d > 0)
     def _():
-        keep_on.wait_recv()
-
-    @pl.when(even)
-    def _():
-        keep_back.wait_recv()
-
-    def relay(r):
-        h = theirs + r
-
-        @pl.when(gets_early)
-        def _():
-            a_copy(r).wait_recv()
-
-        @pl.when((d + 2 < ctx_size) & even)
-        def _():
-            sout[r] = (arecv[r].astype(F32) + kmate[pl.ds(h, 1), :] * own[r]).astype(BF16)
-            s_copy(r).start()
-
-        @pl.when((d + 2 < ctx_size) & odd)
-        def _():
-            sout[r] = (own[r] + kown[pl.ds(h, 1), :] * arecv[r].astype(F32)).astype(BF16)
-            s_copy(r).start()
-
-    def pass_on(r):
-        @pl.when(d >= 2)
-        def _():
-            s_copy(r).wait_recv()
-
-        @pl.when(even)
-        def _():
-            lsend[r] = (own[r] + kown[pl.ds(theirs + r, 1), :] * srecv[r].astype(F32)).astype(BF16)
-            f_copy(r).start()
-
-        @pl.when(odd & (d >= 2))
-        def _():
-            g_copy(r).start()
-
-    @pl.when(d > 0)
-    def _():
-        halo_p.wait_recv()
-        halo_f.wait_recv()
-
-    xp[:8, :] = prim[...].astype(F32)
+        halo.wait_recv()
+
+    xp[:8, :] = rim[:, cols // 2 :].astype(F32)
     bc[:16, :] = tap_sum(
         lambda lag: xp[8 - lag : 24 - lag, :], ptaps_ref[...], pbias_ref[...], offs[:16, :1], taps_n
     ).astype(BF16)
     for c in range(cols // 512):
         sl = slice(c * 512, (c + 1) * 512)
-        xs[:8, sl] = rim[:, sl].astype(F32)
+        first = c * 512 < cols // 2
+        arrived = rim[:, (c * 512) % (cols // 2) : (c * 512) % (cols // 2) + 512].astype(F32)
+        xs[:8, sl] = jnp.concatenate([arrived[:4], arrived[:4]], axis=0) if first else arrived
         conv[:16, sl] = tap_sum(
             lambda lag: xs[8 - lag : 24 - lag, sl], taps_ref[:, sl], bias_ref[:, sl], offs[:16, :1], taps_n
         ).astype(BF16)
@@ -448,10 +460,8 @@
     gap = ti - si
     masked[...] = jnp.where((gap >= 0) & (offs[:, :1] >= gap.astype(F32)), scores, 0.0)
 
-    def local_part(c):
-        gate_copy(c).wait()
-        for k in range(pair):
-            h = c * pair + k
+    def local_part(h):
+        for _ in range(1):
             fcols = cols_of(h, 1)
             arow = a_rows[pl.ds(h, 1), :]
             cbv = cb[h]
@@ -522,31 +532,32 @@
         return 0
 
     def second_body(i, _):
-        relay(i)
-        local_part(i)
         pass_on(i - lag)
+        local_part(part_heads + i - lag)
         return 0
 
-    lax.fori_loop(0, lag, first_body, 0)
-    lax.fori_loop(lag, part_heads, second_body, 0)
+    def both_body(i, _):
+        first_body(i, 0)
+        second_body(i, 0)
+        return 0
+
+    gate_copy.wait()
+    for r in range(ready):
+        local_part(r)
+    lax.fori_loop(ready, lag, first_body, 0)
+    lax.fori_loop(lag, part_heads, both_body, 0)
+    lax.fori_loop(part_heads, part_heads + lag, second_body, 0)
     early_terms()
-    done = 0
-    for r in range(part_heads - lag, part_heads):
-        pass_on(r)
-        if done + pair <= r + 1:
-            finish_theirs(done)
-            done += pair
-    while done < part_heads:
-        finish_theirs(done)
-        done += pair
+    for r in range(0, part_heads, pair):
+        finish_theirs(r)
 
     def last_body(j, _):
         r = j * pair
 
         @pl.when(gets_late)
         def _():
-            for k in range(pair):
-                f_copy(r + k).wait_recv()
+            some = pl.ds(r, pair)
+            remote(lsend.at[some], lrecv.at[some], fsend, lrecv_sem.at[j], (mate, hd)).wait_recv()
 
         finish(parity, r, jnp.concatenate([lrecv[r + k] for k in range(pair)], axis=1))
         return 0
@@ -557,7 +568,7 @@
 
     def sq_copy(k):
         return remote(
-            sq, sqr.at[k - 1], sqsend.at[k - 1], sqrecv.at[k - 1], (d, lax.rem(hd + k, head_size))
+            sq, sqr.at[k - 1], sqsend, sqrecv.at[k - 1], (d, lax.rem(hd + k, head_size))
         )
 
     for k in range(1, head_size):
@@ -565,8 +576,7 @@
 
     @pl.when(d + 1 < ctx_size)
     def _():
-        halo_p.wait_send()
-        halo_f.wait_send()
+        halo.wait_send()
         keep_on.wait_send()
         top_one.wait_send()
 
@@ -578,30 +588,25 @@
     def _():
         keep_back.wait_send()
 
-    def drain(r, _):
-        @pl.when(sends_early)
-        def _():
-            a_copy(r).wait_send()
-
-        @pl.when(d + 2 < ctx_size)
-        def _():
-            s_copy(r).wait_send()
-
-        @pl.when(sends_late)
-        def _():
-            f_copy(r).wait_send()
-
-        return 0
-
-    lax.fori_loop(0, part_heads, drain, 0)
+    @pl.when(sends_early)
+    def _():
+        remote(send, arecv, asend, arecv_sem.at[0], (mate, hd)).wait_send()
+
+    @pl.when(d + 2 < ctx_size)
+    def _():
+        remote(sout, srecv, ssend, srecv_sem.at[0], (d + 2, hd)).wait_send()
+
+    @pl.when(sends_late)
+    def _():
+        remote(lsend, lrecv, fsend, lrecv_sem.at[0], (mate, hd)).wait_send()
+
     total = sq[...]
     for k in range(1, head_size):
         sq_copy(k).wait_recv()
         total = total + sqr[k - 1]
     scale = lax.rsqrt(total / (cols * head_size) + 1e-05)
     scale_ref[...] = jnp.broadcast_to(scale, (hdim, rows)).T
-    for k in range(1, head_size):
-        sq_copy(k).wait_send()
+    remote(sqr, sqr, sqsend, sqrecv.at[0], (d, lax.rem(hd + 1, head_size))).wait_send()
 
 
 def scale_kernel(gated_ref, scale_ref, gain_ref, out_hbm, staged, sems):
@@ -677,7 +682,7 @@
             V((1, heads), F32),
             V((rows, cols), BF16), V((rows, cols), BF16), V((rows, 2 * state), BF16),
             V((rows + 8, cols), F32), V((rows + 8, 2 * state), F32),
-            V((8, cols), BF16), V((8, 2 * state), BF16), V((rows, cols), BF16),
+            V((8, cols // 2 + 2 * state), BF16), V((rows, cols), BF16),
             V((state, rows), F32), V((rows, 2 * state), BF16), V((rows, state), BF16), V((rows, rows), F32),
             V((heads, rows, hdim), F32), V((heads, rows), F32), V((heads, rows), F32), V((heads, hdim), F32),
             V((rows, hdim), F32), V((heads, hdim), F32),
@@ -687,10 +692,11 @@
             V((8, state + cols // 2), BF16), V((2, 8, state + cols // 2), BF16), V((2, rows, 16), BF16),
             V((16, cols // 2), BF16),
             V((rows, cols), F32), V((rows, cols), F32), V((rows, hdim), F32),
-            V((1, rows), F32), V((head_size - 1, 1, rows), F32),
-            DMA((10,)), DMA((chunks,)), DMA((chunks,)), *[DMA((2,)) for _ in range(6)],
-            *[DMA((some,)) for _ in range(6)],
-            DMA((head_size - 1,)), DMA((head_size - 1,)),
+            V((1, rows), F32), V((head_size - 1, 1, rows), F32), V((8, cols), BF16), V((8, 2 * state), BF16),
+            V((8, cols // 2 + 2 * state), BF16), DMA((2,)),
+            DMA((10,)), DMA((chunks,)), DMA, DMA, DMA, *[DMA((2,)) for _ in range(4)],
+            DMA, DMA((some,)), DMA, DMA((some,)), DMA, DMA((chunks // 2,)),
+            DMA, DMA((head_size - 1,)),
         ],
         compiler_params=pltpu.CompilerParams(collective_id=0, has_side_effects=True, vmem_limit_bytes=40 << 20),
         name="mixer",

time: 24 us -> 22.9 us (0.954)
  Pallas kernels: 23.8 us -> 22.7 us
    pallas_call x1, Pallas kernels: 22.8 us -> 21.6 us  [short_body(): pl.pallas_call(functools.partial(mixer_kernel, ctx_size, head_size, pair)...]
where the time goes in v3:
time: 22.9 us; the launch traced here: 22.7 us
  Pallas kernels  22.7 us (99%)
    pallas_call x1, Pallas kernels, short_body(): pl.pallas_call(functools.partial(mixer_kernel, ctx_size, head_size, pair)...  21.6 us
    pallas_call x1, Pallas kernels, finish_call(): pl.pallas_call(scale_kernel, out_shape=jax.ShapeDtypeStruct((rows, cols),...  1.06 us

profile of v3, /device:TPU:9, one launch (start us, length us, event | category | flops | bytes accessed | tf_op | source)
XLA Modules:
  0.0 22.7 jit_solution(6964778754406800705)
XLA Ops:
  0.0 0.0 copy-start
  0.0 21.6 %mixer.1 = (bf16[256,2048]{1,0:T(8,128)(2,1)S(1)}, f32[256,128]{1,0:T(8,128)S(1)}) custom-call(bf16[256,2048]{1,0:T(8,128)(2,1)} %feat_hbm.1, bf16[256,2048]{1,0:T(8,128)(2,1)} %gate_hbm.1, bf16[256,256]{1,0:T(8,128)(2,1)} %proj_hbm.1, f32[16,256]{1,0:T(8,128)} %step_hbm.1, s32[1,256]{1,0:T(1,128)} %bitcast.9, f32[4,2048]{1,0:T(4,128)} %taps_hbm.1, ...), custom_call_target="tpu_custom_call" | custom-call | tf_op jit(solution)/shard_map/mixer/pallas_call | solution.py:671
  21.7 0.0 copy-done
  21.7 1.1 %scale.1 = bf16[256,2048]{1,0:T(8,128)(2,1)} custom-call(bf16[256,2048]{1,0:T(8,128)(2,1)S(1)} %get-tuple-element.7.gated_ref, f32[256,128]{1,0:T(8,128)S(1)} %get-tuple-element.8.scale_ref, f32[1,2048]{1,0:T(1,128)S(1)} %bitcast.7), custom_call_target="tpu_custom_call" | custom-call | tf_op jit(solution)/shard_map/scale/pallas_call | solution.py:635
Async XLA Ops:
  0.0 21.7 %copy-start = (f32[2048]{0:T(1024)S(1)}, f32[2048]{0:T(1024)}, u32[]{:S(2)}) copy-start(f32[2048]{0:T(1024)} %param.25) | copy-start | bytes 24580

commit v4 on v3

--- a/solution.py
+++ b/solution.py
@@ -134,8 +134,9 @@
 
 
 PAIR = 2
-READY = 2
-LAG = 5
+HOLD = 1
+AHEAD = 2
+EARLY = 4
 STRIPE = 32
 
 LOG2E = 1.4426950408889634
@@ -196,11 +197,17 @@
     odd = d % 2 == 1
     even = d % 2 == 0
     parity = d % 2
+    first_core = hd % 2 == 0
     mate = d + 1 - 2 * parity
     part_heads = heads // 2
     part_chunks = chunks // 2
     mine = parity * part_heads
     theirs = part_heads - mine
+    cross = pair if part_heads > 2 * pair else 0
+    single = part_heads - cross
+    single_chunks = single // pair
+    moved = single + 2 * cross
+    moved_chunks = moved // pair
     sends_early = even | (d + 1 < ctx_size)
     gets_early = odd | (d + 2 < ctx_size)
     sends_late = even | (d >= 2)
@@ -233,8 +240,15 @@
             barrier, inc=1, device_id=(d, lax.rem(hd + k, head_size)), device_id_type=pl.DeviceIdType.MESH
         )
 
+    def cross_chunk(j):
+        return j * part_chunks + single_chunks
+
     def ordered(i):
-        return lax.rem(mine // pair + i, chunks)
+        if i < single_chunks:
+            return mine // pair + i
+        if i < moved_chunks:
+            return cross_chunk(i - single_chunks)
+        return theirs // pair + i - moved_chunks
 
     tail_copies = [
         pltpu.make_async_copy(feat_hbm.at[pl.ds(rows - 8, 8), :], tail, tail_sems.at[0]),
@@ -287,6 +301,18 @@
     tail_half[:, : cols // 2] = jnp.concatenate(
         [tail[:, : cols // 2].astype(F32)[4:], tail[:, cols // 2 :].astype(F32)[4:]], axis=0
     ).astype(BF16)
+    def proj_taps(rows_from, rows_to, cs):
+        return tap_sum(
+            lambda lag: xp[8 + rows_from - lag : 8 + rows_to - lag, cs], ptaps_ref[:, cs], pbias_ref[:, cs],
+            offs[rows_from:rows_to, :1], taps_n,
+        ).astype(BF16)
+
+    in_cols, out_cols = slice(0, state), slice(state, 2 * state)
+    for copy in small[4:]:
+        copy.wait()
+    xp[8:, :] = proj[...].astype(F32)
+    bc[:, in_cols] = proj_taps(0, rows, in_cols)
+    in_t[...] = bc[:, in_cols].astype(F32).T
     near = jnp.minimum(d, 2) + jnp.minimum(ctx_size - 1 - d, 2) + head_size - 1
     pl.semaphore_wait(barrier, near)
     halo = remote(tail_half, rim, halo_send, halo_recv, (d + 1, hd))
@@ -315,6 +341,9 @@
     def a_copy(r):
         return remote(send.at[r], arecv.at[r], asend, arecv_sem.at[r], (mate, hd))
 
+    def direct_copy(r):
+        return remote(send.at[r], srecv.at[r], ssend, srecv_sem.at[r], (d + 2, hd))
+
     def s_copy(r):
         return remote(sout.at[r], srecv.at[r], ssend, srecv_sem.at[r], (d + 2, hd))
 
@@ -328,33 +357,55 @@
         scaled = (in_t[...] * coef[pl.ds(h, 1), :]).astype(BF16)
         return jnp.dot(scaled, conv[:, cols_of(h, 1)], preferred_element_type=F32)
 
-    def mine_body(i, _):
-        conv_all(mine // pair + i)
+    def held_back(i):
+        @pl.when((i >= 0) & (i < moved_chunks) & sends_early & jnp.logical_not(first_core))
+        def _():
+            for k in range(pair):
+                a_copy(i * pair + k).start()
+
+    def sent(c, slot, keeps):
+        conv_all(c)
         for k in range(pair):
-            r = i * pair + k
-            send[r] = contrib(mine + r).astype(BF16)
-
-            @pl.when(sends_early)
+            r = slot * pair + k
+            got = contrib(c * pair + k)
+            send[r] = got.astype(BF16)
+            if keeps:
+                own[r] = got
+
+            @pl.when(sends_early & first_core)
             def _():
                 a_copy(r).start()
 
+            if keeps:
+                @pl.when(odd & (d + 2 < ctx_size))
+                def _():
+                    direct_copy(r).start()
+
+        held_back(slot - HOLD)
+
+    def mine_body(i, _):
+        sent(mine // pair + i, i, False)
         return 0
 
+    def cross_body(i, _):
+        sent(cross_chunk(i), single_chunks + i, True)
+        return 0
+
     def theirs_body(i, _):
+        held_back(moved_chunks + i - HOLD)
         conv_all(theirs // pair + i)
         for k in range(pair):
             r = i * pair + k
             own[r] = contrib(theirs + r)
+
+        @pl.when(odd & (i >= 1) & (i <= AHEAD))
+        def _():
+            relay(i - 1)
+
         return 0
 
-    for copy in small[4:]:
-        copy.wait()
-    xp[8:, :] = proj[...].astype(F32)
-    bc[...] = tap_sum(
-        lambda lag: xp[8 - lag : 8 + rows - lag, :], ptaps_ref[...], pbias_ref[...], offs[:, :1], taps_n
-    ).astype(BF16)
-    in_t[...] = bc[:, :state].astype(F32).T
-    lax.fori_loop(0, part_chunks, mine_body, 0)
+    lax.fori_loop(0, single_chunks, mine_body, 0)
+    lax.fori_loop(0, moved_chunks - single_chunks, cross_body, 0)
 
     @pl.when(d == 0)
     def _():
@@ -368,7 +419,6 @@
         srecv[...] = jnp.zeros_like(srecv)
         tin[1] = jnp.zeros(tin.shape[1:], BF16)
 
-    lax.fori_loop(0, part_chunks, theirs_body, 0)
 
     @pl.when(d > 0)
     def _():
@@ -409,12 +459,19 @@
         def _():
             g_copy(r).start()
 
-    ready = min(READY, part_heads)
+    ahead = jnp.where(odd, min(AHEAD, single_chunks - 1), 0)
+    lax.fori_loop(0, single_chunks, theirs_body, 0)
+    cum_t = cum.T
+
+    def spread(some):
+        for h in some:
+            cb[h] = jnp.broadcast_to(cum_t[:, h : h + 1], (rows, hdim))
+
+    fill = [lambda: spread(range(part_heads)), lambda: spread(range(part_heads, heads))]
+    ready = len(fill)
     for r in range(ready):
-        relay(r)
-    cum_t = cum.T
-    for h in range(heads):
-        cb[h] = jnp.broadcast_to(cum_t[:, h : h + 1], (rows, hdim))
+        relay(ahead + r)
+        fill[r]()
     skips[...] = jnp.broadcast_to(to_column(skip_ref[...], heads), skips.shape)
 
     @pl.when(d > 0)
@@ -422,9 +479,8 @@
         halo.wait_recv()
 
     xp[:8, :] = rim[:, cols // 2 :].astype(F32)
-    bc[:16, :] = tap_sum(
-        lambda lag: xp[8 - lag : 24 - lag, :], ptaps_ref[...], pbias_ref[...], offs[:16, :1], taps_n
-    ).astype(BF16)
+    bc[:16, in_cols] = proj_taps(0, 16, in_cols)
+    out_b[...] = proj_taps(0, rows, out_cols)
     for c in range(cols // 512):
         sl = slice(c * 512, (c + 1) * 512)
         first = c * 512 < cols // 2
@@ -452,8 +508,7 @@
     def _():
         top_two.start()
 
-    in_b = bc[:, :state]
-    out_b[...] = bc[:, state:]
+    in_b = bc[...]
     scores = lax.dot_general(out_b[...], in_b, (((1,), (1,)), ((), ())), preferred_element_type=F32)
     ti = lax.broadcasted_iota(jnp.int32, (rows, rows), 0)
     si = lax.broadcasted_iota(jnp.int32, (rows, rows), 1)
@@ -512,47 +567,96 @@
             total = total + squares[:, k * hdim : (k + 1) * hdim]
         part[...] += total
 
-    def finish_theirs(r):
+    def finish_received(r, side_even, side_odd, row):
         @pl.when(even)
         def _():
-            finish(1, r, jnp.concatenate([srecv[r + k] for k in range(pair)], axis=1))
+            finish(side_even, row, jnp.concatenate([srecv[r + k] for k in range(pair)], axis=1))
 
         @pl.when(odd)
         def _():
-            finish(0, r, jnp.concatenate([
-                (arecv[r + k].astype(F32) + kprev[pl.ds(r + k, 1), :] * srecv[r + k].astype(F32)).astype(BF16)
+            finish(side_odd, row, jnp.concatenate([
+                (
+                    arecv[r + k].astype(F32)
+                    + kprev[side_odd * part_heads + row + k : side_odd * part_heads + row + k + 1, :]
+                    * srecv[r + k].astype(F32)
+                ).astype(BF16)
                 for k in range(pair)
             ], axis=1))
 
-    lag = min(LAG, part_heads)
+    begun = ahead + ready
+    early = min(EARLY, single)
 
     def first_body(i, _):
         relay(i)
-        local_part(i)
+        local_part(i - begun)
         return 0
 
+    def both_body(i, _):
+        local_part(i - begun)
+        pass_on(i - early)
+        relay(i)
+        return 0
+
+    def cross_relay(x):
+        r = single + x
+
+        @pl.when(gets_early)
+        def _():
+            a_copy(r).wait_recv()
+
+        @pl.when((d + 2 < ctx_size) & even)
+        def _():
+            h = x // pair * part_heads + single + x % pair
+            sout[r] = (arecv[r].astype(F32) + kmate[pl.ds(h, 1), :] * own[r]).astype(BF16)
+            s_copy(r).start()
+
     def second_body(i, _):
-        pass_on(i - lag)
-        local_part(part_heads + i - lag)
+        for k in range(2):
+            h = single - begun + 2 * (i - single + early) + k
+
+            @pl.when(h < heads)
+            def _():
+                local_part(h)
+
+            if k == 0:
+                pass_on(i)
+
+        x = i - single + early
+
+        @pl.when(x < moved - single)
+        def _():
+            cross_relay(x)
+
         return 0
 
-    def both_body(i, _):
-        first_body(i, 0)
-        second_body(i, 0)
+    def left_body(h, _):
+        local_part(h)
         return 0
 
     gate_copy.wait()
-    for r in range(ready):
-        local_part(r)
-    lax.fori_loop(ready, lag, first_body, 0)
-    lax.fori_loop(lag, part_heads, both_body, 0)
-    lax.fori_loop(part_heads, part_heads + lag, second_body, 0)
+    lax.fori_loop(begun, early, first_body, 0)
+    lax.fori_loop(early, single, both_body, 0)
+    lax.fori_loop(single - early, single, second_body, 0)
+    lax.fori_loop(single - begun + 2 * early, heads, left_body, 0)
+    for x in range(early, moved - single):
+        cross_relay(x)
     early_terms()
-    for r in range(0, part_heads, pair):
-        finish_theirs(r)
-
-    def last_body(j, _):
+    for r in range(0, single, pair):
+        finish_received(r, 1, 0, r)
+
+    for j in range(single_chunks):
         r = j * pair
+
+        if j == single_chunks - 1:
+            for x in range((moved - single) // pair):
+                at = single + x * pair
+
+                @pl.when(d >= 2)
+                def _():
+                    for k in range(pair):
+                        s_copy(at + k).wait_recv()
+
+                finish_received(at, x, x, single)
 
         @pl.when(gets_late)
         def _():
@@ -560,9 +664,6 @@
             remote(lsend.at[some], lrecv.at[some], fsend, lrecv_sem.at[j], (mate, hd)).wait_recv()
 
         finish(parity, r, jnp.concatenate([lrecv[r + k] for k in range(pair)], axis=1))
-        return 0
-
-    lax.fori_loop(0, part_chunks, last_body, 0)
 
     sq[...] = jnp.sum(part[...].T, axis=0, keepdims=True)
 
@@ -594,7 +695,7 @@
 
     @pl.when(d + 2 < ctx_size)
     def _():
-        remote(sout, srecv, ssend, srecv_sem.at[0], (d + 2, hd)).wait_send()
+        remote(send, srecv, ssend, srecv_sem.at[0], (d + 2, hd)).wait_send()
 
     @pl.when(sends_late)
     def _():
@@ -663,7 +764,11 @@
     hbm = pl.BlockSpec(memory_space=pltpu.HBM)
     V = pltpu.VMEM
     DMA = pltpu.SemaphoreType.DMA
-    piece = (some, state, hdim)
+    cross = pair if some > 2 * pair else 0
+    single = some - cross
+    moved = single + 2 * cross
+    late_piece = (single, state, hdim)
+    piece = (moved, state, hdim)
     operands = (
         feat_in, gate_in, state_proj, step_raw, doc_offset[None, :], feat_taps,
         feat_bias[None, :], proj_taps, proj_bias[None, :], step_bias[None, :], decay_log[None, :], skip_gain[None, :],
@@ -683,11 +788,11 @@
             V((rows, cols), BF16), V((rows, cols), BF16), V((rows, 2 * state), BF16),
             V((rows + 8, cols), F32), V((rows + 8, 2 * state), F32),
             V((8, cols // 2 + 2 * state), BF16), V((rows, cols), BF16),
-            V((state, rows), F32), V((rows, 2 * state), BF16), V((rows, state), BF16), V((rows, rows), F32),
+            V((state, rows), F32), V((rows, state), BF16), V((rows, state), BF16), V((rows, rows), F32),
             V((heads, rows, hdim), F32), V((heads, rows), F32), V((heads, rows), F32), V((heads, hdim), F32),
             V((rows, hdim), F32), V((heads, hdim), F32),
-            V(piece, F32), V(piece, BF16), V(piece, BF16), V(piece, BF16), V(piece, BF16), V(piece, BF16),
-            V(piece, BF16),
+            V(piece, F32), V(piece, BF16), V(piece, BF16), V(piece, BF16), V(piece, BF16), V(late_piece, BF16),
+            V(late_piece, BF16),
             V((heads, hdim), F32), V((heads, hdim), F32), V((heads, hdim), F32),
             V((8, state + cols // 2), BF16), V((2, 8, state + cols // 2), BF16), V((2, rows, 16), BF16),
             V((16, cols // 2), BF16),
@@ -695,7 +800,7 @@
             V((1, rows), F32), V((head_size - 1, 1, rows), F32), V((8, cols), BF16), V((8, 2 * state), BF16),
             V((8, cols // 2 + 2 * state), BF16), DMA((2,)),
             DMA((10,)), DMA((chunks,)), DMA, DMA, DMA, *[DMA((2,)) for _ in range(4)],
-            DMA, DMA((some,)), DMA, DMA((some,)), DMA, DMA((chunks // 2,)),
+            DMA, DMA((moved,)), DMA, DMA((moved,)), DMA, DMA((single // pair,)),
             DMA, DMA((head_size - 1,)),
         ],
         compiler_params=pltpu.CompilerParams(collective_id=0, has_side_effects=True, vmem_limit_bytes=40 << 20),

time: 22.9 us -> 22.2 us (0.969)
  Pallas kernels: 22.7 us -> 22 us
    pallas_call x1, Pallas kernels: 21.6 us -> 21 us  [short_body(): pl.pallas_call(functools.partial(mixer_kernel, ctx_size, head_size, pair)...]
where the time goes in v4:
time: 22.2 us; the launch traced here: 22 us
  Pallas kernels  22 us (99%)
    pallas_call x1, Pallas kernels, short_body(): pl.pallas_call(functools.partial(mixer_kernel, ctx_size, head_size, pair)...  21 us
    pallas_call x1, Pallas kernels, finish_call(): pl.pallas_call(scale_kernel, out_shape=jax.ShapeDtypeStruct((rows, cols),...  1.06 us

profile of v4, /device:TPU:9, one launch (start us, length us, event | category | flops | bytes accessed | tf_op | source)
XLA Modules:
  0.0 22.0 jit_solution(13196155146696265980)
XLA Ops:
  0.0 0.0 copy-start
  0.0 21.0 %mixer.1 = (bf16[256,2048]{1,0:T(8,128)(2,1)S(1)}, f32[256,128]{1,0:T(8,128)S(1)}) custom-call(bf16[256,2048]{1,0:T(8,128)(2,1)} %feat_hbm.1, bf16[256,2048]{1,0:T(8,128)(2,1)} %gate_hbm.1, bf16[256,256]{1,0:T(8,128)(2,1)} %proj_hbm.1, f32[16,256]{1,0:T(8,128)} %step_hbm.1, s32[1,256]{1,0:T(1,128)} %bitcast.9, f32[4,2048]{1,0:T(4,128)} %taps_hbm.1, ...), custom_call_target="tpu_custom_call" | custom-call | tf_op jit(solution)/shard_map/mixer/pallas_call | solution.py:776
  21.0 0.0 copy-done
  21.0 1.1 %scale.1 = bf16[256,2048]{1,0:T(8,128)(2,1)} custom-call(bf16[256,2048]{1,0:T(8,128)(2,1)S(1)} %get-tuple-element.7.gated_ref, f32[256,128]{1,0:T(8,128)S(1)} %get-tuple-element.8.scale_ref, f32[1,2048]{1,0:T(1,128)S(1)} %bitcast.7), custom_call_target="tpu_custom_call" | custom-call | tf_op jit(solution)/shard_map/scale/pallas_call | solution.py:736
Async XLA Ops:
  0.0 21.0 %copy-start = (f32[2048]{0:T(1024)S(1)}, f32[2048]{0:T(1024)}, u32[]{:S(2)}) copy-start(f32[2048]{0:T(1024)} %param.25) | copy-start | bytes 24580

commit v5 on v4

--- a/solution.py
+++ b/solution.py
@@ -180,8 +180,7 @@
     feat, gate, proj, xs, xp, rim, conv, in_t, bc, out_b, masked, cb, a_rows, coef, coef_top,
     offs, skips, own, send, arecv, srecv, sout, lsend, lrecv, kown, kmate, kprev,
     top, tin, ext, xt, yv, g2, part, sq, sqr, tail, tail_proj, tail_half, tail_sems,
-    small_sems, feat_sems, gate_sem, halo_send, halo_recv, keep_send, keep_recv, top_send, top_recv,
-    asend, arecv_sem, ssend, srecv_sem, fsend, lrecv_sem, sqsend, sqrecv,
+    small_sems, feat_sems, halo_recv, keep_recv, top_recv, arecv_sem, srecv_sem, lrecv_sem, sqrecv,
 ):
     d = lax.axis_index("ctx")
     hd = lax.axis_index("head")
@@ -213,6 +212,10 @@
     sends_late = even | (d >= 2)
     gets_late = odd | (d >= 2)
 
+    halo_send, keep_send, top_send = small_sems.at[0], small_sems.at[pl.ds(1, 2)], small_sems.at[pl.ds(3, 2)]
+    asend, ssend, fsend, sqsend = (small_sems.at[n] for n in range(5, 9))
+    gate_sem = small_sems.at[9]
+
     def cols_of(h, count):
         return pl.ds(pl.multiple_of(h * hdim, hdim), count * hdim)
 
@@ -268,7 +271,6 @@
         copy.start()
     for c in range(chunks):
         feat_copy(ordered(c)).start()
-    gate_copy.start()
 
     xs[:8, :] = jnp.zeros((8, cols), F32)
     xp[:8, :] = jnp.zeros((8, 2 * state), F32)
@@ -315,6 +317,7 @@
     in_t[...] = bc[:, in_cols].astype(F32).T
     near = jnp.minimum(d, 2) + jnp.minimum(ctx_size - 1 - d, 2) + head_size - 1
     pl.semaphore_wait(barrier, near)
+    gate_copy.start()
     halo = remote(tail_half, rim, halo_send, halo_recv, (d + 1, hd))
     keep_on = remote(kown, kprev, keep_send.at[0], keep_recv.at[0], (d + 1, hd))
     keep_back = remote(kown, kmate, keep_send.at[1], keep_recv.at[1], (d - 1, hd))
@@ -338,6 +341,13 @@
             lambda lag: xs[8 - lag : 8 + rows - lag, sl], taps_ref[:, sl], bias_ref[:, sl], offs[:, :1], taps_n
         ).astype(BF16)
 
+    def conv_head(h):
+        sl = cols_of(h, 1)
+        xs[8:, sl] = feat[:, sl].astype(F32)
+        conv[:, sl] = tap_sum(
+            lambda lag: xs[8 - lag : 8 + rows - lag, sl], taps_ref[:, sl], bias_ref[:, sl], offs[...], taps_n
+        ).astype(BF16)
+
     def a_copy(r):
         return remote(send.at[r], arecv.at[r], asend, arecv_sem.at[r], (mate, hd))
 
@@ -347,11 +357,15 @@
     def s_copy(r):
         return remote(sout.at[r], srecv.at[r], ssend, srecv_sem.at[r], (d + 2, hd))
 
+    def late_sem(r):
+        whole = single - pair
+        return lrecv_sem.at[jnp.where(r < whole, r // pair, whole // pair + r - whole)]
+
     def f_copy(r):
-        return remote(lsend.at[r], lrecv.at[r], fsend, lrecv_sem.at[r // pair], (mate, hd))
+        return remote(lsend.at[r], lrecv.at[r], fsend, late_sem(r), (mate, hd))
 
     def g_copy(r):
-        return remote(srecv.at[r], lrecv.at[r], fsend, lrecv_sem.at[r // pair], (mate, hd))
+        return remote(srecv.at[r], lrecv.at[r], fsend, late_sem(r), (mate, hd))
 
     def contrib(h):
         scaled = (in_t[...] * coef[pl.ds(h, 1), :]).astype(BF16)
@@ -364,9 +378,10 @@
                 a_copy(i * pair + k).start()
 
     def sent(c, slot, keeps):
-        conv_all(c)
+        feat_copy(c).wait()
         for k in range(pair):
             r = slot * pair + k
+            conv_head(c * pair + k)
             got = contrib(c * pair + k)
             send[r] = got.astype(BF16)
             if keeps:
@@ -555,15 +570,15 @@
                 [tin[0, :, cs].astype(F32), tin[1, :, cs].astype(F32) * decay], axis=0
             ).astype(BF16)
 
-    def finish(side, r, st):
-        sl = cols_of(side * part_heads + r, pair)
+    def finish(side, r, st, count=pair):
+        sl = cols_of(side * part_heads + r, count)
         fs = jnp.dot(out_b[...], st, preferred_element_type=F32)
-        fs = fs + jnp.dot(ext[side], xt[:, cols_of(r, pair)], preferred_element_type=F32)
+        fs = fs + jnp.dot(ext[side], xt[:, cols_of(r, count)], preferred_element_type=F32)
         gt = yv[:, sl] + fs * g2[:, sl]
         gated[:, sl] = gt.astype(gated.dtype)
         squares = gt * gt
         total = squares[:, :hdim]
-        for k in range(1, pair):
+        for k in range(1, count):
             total = total + squares[:, k * hdim : (k + 1) * hdim]
         part[...] += total
 
@@ -658,12 +673,19 @@
 
                 finish_received(at, x, x, single)
 
-        @pl.when(gets_late)
-        def _():
-            some = pl.ds(r, pair)
-            remote(lsend.at[some], lrecv.at[some], fsend, lrecv_sem.at[j], (mate, hd)).wait_recv()
-
-        finish(parity, r, jnp.concatenate([lrecv[r + k] for k in range(pair)], axis=1))
+            for k in range(pair):
+                @pl.when(gets_late)
+                def _():
+                    f_copy(r + k).wait_recv()
+
+                finish(parity, r + k, lrecv[r + k], 1)
+        else:
+            @pl.when(gets_late)
+            def _():
+                some = pl.ds(r, pair)
+                remote(lsend.at[some], lrecv.at[some], fsend, lrecv_sem.at[j], (mate, hd)).wait_recv()
+
+            finish(parity, r, jnp.concatenate([lrecv[r + k] for k in range(pair)], axis=1))
 
     sq[...] = jnp.sum(part[...].T, axis=0, keepdims=True)
 
@@ -672,7 +694,8 @@
             sq, sqr.at[k - 1], sqsend, sqrecv.at[k - 1], (d, lax.rem(hd + k, head_size))
         )
 
-    for k in range(1, head_size):
+    far_first = sorted(range(1, head_size), key=lambda k: (k != head_size // 2, k))
+    for k in far_first:
         sq_copy(k).start()
 
     @pl.when(d + 1 < ctx_size)
@@ -799,9 +822,8 @@
             V((rows, cols), F32), V((rows, cols), F32), V((rows, hdim), F32),
             V((1, rows), F32), V((head_size - 1, 1, rows), F32), V((8, cols), BF16), V((8, 2 * state), BF16),
             V((8, cols // 2 + 2 * state), BF16), DMA((2,)),
-            DMA((10,)), DMA((chunks,)), DMA, DMA, DMA, *[DMA((2,)) for _ in range(4)],
-            DMA, DMA((moved,)), DMA, DMA((moved,)), DMA, DMA((single // pair,)),
-            DMA, DMA((head_size - 1,)),
+            DMA((10,)), DMA((chunks,)), DMA, DMA((2,)), DMA((2,)),
+            DMA((moved,)), DMA((moved,)), DMA((single // pair + pair - 1,)), DMA((head_size - 1,)),
         ],
         compiler_params=pltpu.CompilerParams(collective_id=0, has_side_effects=True, vmem_limit_bytes=40 << 20),
         name="mixer",

time: 22.2 us -> 22 us (level)
  no operation moved by 1% of the time
where the time goes in v5:
time: 22 us; the launch traced here: 21.9 us
  Pallas kernels  21.8 us (99%)
    pallas_call x1, Pallas kernels, short_body(): pl.pallas_call(functools.partial(mixer_kernel, ctx_size, head_size, pair)...  20.8 us
    pallas_call x1, Pallas kernels, finish_call(): pl.pallas_call(scale_kernel, out_shape=jax.ShapeDtypeStruct((rows, cols),...  1.06 us

profile of v5, /device:TPU:9, one launch (start us, length us, event | category | flops | bytes accessed | tf_op | source)
XLA Modules:
  0.0 21.9 jit_solution(957807047441560071)
XLA Ops:
  0.0 0.0 copy-start
  0.0 20.8 %mixer.1 = (bf16[256,2048]{1,0:T(8,128)(2,1)S(1)}, f32[256,128]{1,0:T(8,128)S(1)}) custom-call(bf16[256,2048]{1,0:T(8,128)(2,1)} %feat_hbm.1, bf16[256,2048]{1,0:T(8,128)(2,1)} %gate_hbm.1, bf16[256,256]{1,0:T(8,128)(2,1)} %proj_hbm.1, f32[16,256]{1,0:T(8,128)} %step_hbm.1, s32[1,256]{1,0:T(1,128)} %bitcast.9, f32[4,2048]{1,0:T(4,128)} %taps_hbm.1, ...), custom_call_target="tpu_custom_call" | custom-call | tf_op jit(solution)/shard_map/mixer/pallas_call | solution.py:799
  20.8 0.0 copy-done
  20.8 1.1 %scale.1 = bf16[256,2048]{1,0:T(8,128)(2,1)} custom-call(bf16[256,2048]{1,0:T(8,128)(2,1)S(1)} %get-tuple-element.7.gated_ref, f32[256,128]{1,0:T(8,128)S(1)} %get-tuple-element.8.scale_ref, f32[1,2048]{1,0:T(1,128)S(1)} %bitcast.7), custom_call_target="tpu_custom_call" | custom-call | tf_op jit(solution)/shard_map/scale/pallas_call | solution.py:759
Async XLA Ops:
  0.0 20.8 %copy-start = (f32[2048]{0:T(1024)S(1)}, f32[2048]{0:T(1024)}, u32[]{:S(2)}) copy-start(f32[2048]{0:T(1024)} %param.25) | copy-start | bytes 24580

commit v6 on v5

--- a/solution.py
+++ b/solution.py
@@ -134,7 +134,7 @@
 
 
 PAIR = 2
-HOLD = 1
+HOLD = 0
 AHEAD = 2
 EARLY = 4
 STRIPE = 32

time: 22 us -> 21.9 us (level)
  no operation moved by 1% of the time
where the time goes in v6:
time: 21.9 us; the launch traced here: 21.7 us
  Pallas kernels  21.7 us (99%)
    pallas_call x1, Pallas kernels, short_body(): pl.pallas_call(functools.partial(mixer_kernel, ctx_size, head_size, pair)...  20.6 us
    pallas_call x1, Pallas kernels, finish_call(): pl.pallas_call(scale_kernel, out_shape=jax.ShapeDtypeStruct((rows, cols),...  1.06 us

profile of v6, /device:TPU:9, one launch (start us, length us, event | category | flops | bytes accessed | tf_op | source)
XLA Modules:
  0.0 21.7 jit_solution(14662466324003163061)
XLA Ops:
  0.0 0.0 copy-start
  0.0 20.6 %mixer.1 = (bf16[256,2048]{1,0:T(8,128)(2,1)S(1)}, f32[256,128]{1,0:T(8,128)S(1)}) custom-call(bf16[256,2048]{1,0:T(8,128)(2,1)} %feat_hbm.1, bf16[256,2048]{1,0:T(8,128)(2,1)} %gate_hbm.1, bf16[256,256]{1,0:T(8,128)(2,1)} %proj_hbm.1, f32[16,256]{1,0:T(8,128)} %step_hbm.1, s32[1,256]{1,0:T(1,128)} %bitcast.9, f32[4,2048]{1,0:T(4,128)} %taps_hbm.1, ...), custom_call_target="tpu_custom_call" | custom-call | tf_op jit(solution)/shard_map/mixer/pallas_call | solution.py:799
  20.6 0.0 copy-done
  20.7 1.1 %scale.1 = bf16[256,2048]{1,0:T(8,128)(2,1)} custom-call(bf16[256,2048]{1,0:T(8,128)(2,1)S(1)} %get-tuple-element.7.gated_ref, f32[256,128]{1,0:T(8,128)S(1)} %get-tuple-element.8.scale_ref, f32[1,2048]{1,0:T(1,128)S(1)} %bitcast.7), custom_call_target="tpu_custom_call" | custom-call | tf_op jit(solution)/shard_map/scale/pallas_call | solution.py:759
Async XLA Ops:
  0.0 20.7 %copy-start = (f32[2048]{0:T(1024)S(1)}, f32[2048]{0:T(1024)}, u32[]{:S(2)}) copy-start(f32[2048]{0:T(1024)} %param.25) | copy-start | bytes 24580
